TPU v7x, 512 devices: a whole 4x8x8 slice. The times are simulated.
512 devices in a mesh: row: 32 (over x, y), col: 16 (over z, core).
Axes of the slice: x: 4, y: 8, z: 8, core: 2. Of those that a mesh axis runs over, the one named last changes fastest.
Arguments:
- features: bfloat16 [131072, 128], P(('row', 'col')), may hold values from -6 to 6
- degree: int32 [131072], P(('row', 'col')), may hold values from 1 to 256
- weight: bfloat16 [128, 128], replicated, may hold values from -0.5 to 0.5
- bias: float32 [128], replicated, may hold values from -3 to 3
- cotangent: bfloat16 [131072, 128], P(('row', 'col')), may hold values from -8 to 8
- tile_rows: int32 [32, 16, 128], P('row', 'col'), may hold values from 0 to 31
- tile_cols: int32 [32, 16, 128], P('row', 'col'), may hold values from 0 to 63
- tile_count: int32 [32, 16, 1], P('row', 'col'), may hold values from 32 to 128, as said below
- tile_codes: int32 [32, 16, 128, 256], P('row', 'col'), may hold values from 0 to 4095
Outputs:
- hidden: bfloat16 [131072, 128], P(('row', 'col'))
- grad_features: bfloat16 [131072, 128], P(('row', 'col'))
- grad_weight: float32 [128, 128], replicated
- grad_bias: float32 [128], replicated
Inputs may be any that keep to these rules, and one draw needn't show every extreme that they name: Only the first tile_count slots of a block are live; on some block the count is exactly 128. `tile_rows`: A tile position may repeat within a block; repeated tiles add.
All inputs are finite; a program needn't handle non-finite values.
Results may differ from a plain program's by a relative error of at most 0.019.
Values may be sent and summed in bfloat16 or wider, within the bound.
A program may use at most 64 MiB of HBM per device.

v0:
```python
import math

import jax
import jax.numpy as jnp
from jax import lax
from jax.sharding import PartitionSpec as P

BLOCK = 16


def tile_mask(code_block, living):
    tile_side = code_block.shape[1] // 2
    row_code = code_block[:, :tile_side][:, :, None]
    col_code = code_block[:, tile_side:][:, None, :]
    hashed = (row_code * col_code + row_code + 3 * col_code) % 4093
    return ((hashed < 64) & living[:, None, None]).astype(jnp.bfloat16)


def accumulate(codes_dev, rows_dev, cols_dev, count_dev, source, out_tiles, backward):
    tile_side = source.shape[1]
    width_feat = source.shape[2]

    def block_step(block_id, summed):
        slot_start = block_id * BLOCK
        code_block = lax.dynamic_slice_in_dim(codes_dev, slot_start, BLOCK, 0)
        row_block = lax.dynamic_slice_in_dim(rows_dev, slot_start, BLOCK, 0)
        col_block = lax.dynamic_slice_in_dim(cols_dev, slot_start, BLOCK, 0)
        slot_ids = slot_start + jnp.arange(BLOCK, dtype=jnp.int32)
        target = col_block if backward else row_block
        anchor = row_block if backward else col_block
        living = slot_ids < count_dev
        keep = tile_mask(code_block, living)
        picked = jnp.take(source, anchor, axis=0)
        if backward:
            product = jnp.einsum("tij,tif->tjf", keep, picked, preferred_element_type=jnp.float32)
        else:
            product = jnp.einsum("tij,tjf->tif", keep, picked, preferred_element_type=jnp.float32)
        return summed.at[target].add(product)

    start_sum = jnp.zeros((out_tiles, tile_side, width_feat), jnp.float32)
    loop_count = codes_dev.shape[0] // BLOCK
    summed = lax.fori_loop(0, loop_count, block_step, start_sum)
    return summed.reshape(out_tiles * tile_side, width_feat)


def dense_part(aggregate, weight, bias, cotangent, inv_root):
    preact = jnp.dot(aggregate, weight, preferred_element_type=jnp.float32) + bias
    hidden = jax.nn.elu(preact).astype(jnp.bfloat16)
    elu_slope = jnp.where(preact > 0, 1.0, jnp.exp(jnp.minimum(preact, 0.0)))
    grad_pre = cotangent.astype(jnp.float32) * elu_slope
    grad_pre_b = grad_pre.astype(jnp.bfloat16)
    grad_weight = lax.dot_general(
        aggregate, grad_pre_b, (((0,), (0,)), ((), ())), preferred_element_type=jnp.float32
    )
    grad_bias = jnp.sum(grad_pre, axis=0)
    grad_agg = jnp.dot(grad_pre_b, weight.T, preferred_element_type=jnp.float32)
    grad_scaled = (inv_root * grad_agg).astype(jnp.bfloat16)
    return (hidden, grad_weight, grad_bias, grad_scaled)


def local(features, degree, weight, bias, cotangent, tile_rows, tile_cols, tile_count, tile_codes):
    codes_dev = tile_codes[0, 0]
    rows_dev = tile_rows[0, 0]
    cols_dev = tile_cols[0, 0]
    count_dev = tile_count[0, 0, 0]
    pieces = features.shape[0]
    width_feat = features.shape[1]
    tile_side = codes_dev.shape[1] // 2
    row_devs = lax.axis_size("row")
    col_devs = lax.axis_size("col")
    grad_scale = 1.0 / math.sqrt(pieces * row_devs * col_devs)
    row_tiles = pieces * col_devs // tile_side
    col_tiles = pieces * row_devs // tile_side
    inv_root = lax.rsqrt(degree.astype(jnp.float32))[:, None]
    scaled = (inv_root * features.astype(jnp.float32)).astype(jnp.bfloat16)
    column_feats = lax.all_gather(scaled, "row", axis=0, tiled=True).reshape(
        col_tiles, tile_side, width_feat
    )
    row_terms = accumulate(codes_dev, rows_dev, cols_dev, count_dev, column_feats, row_tiles, False)
    agg_sum = lax.psum_scatter(
        row_terms.astype(jnp.bfloat16), "col", scatter_dimension=0, tiled=True
    ).astype(jnp.float32)
    aggregate = (inv_root * agg_sum).astype(jnp.bfloat16)
    hidden, grad_weight, grad_bias, grad_scaled = dense_part(
        aggregate, weight, bias, cotangent, inv_root
    )
    grad_weight, grad_bias = lax.psum(
        (grad_weight * grad_scale, grad_bias * grad_scale), ("row", "col")
    )
    row_grads = lax.all_gather(grad_scaled, "col", axis=0, tiled=True)
    row_sources = row_grads.reshape(row_tiles, tile_side, width_feat)
    col_terms = accumulate(codes_dev, rows_dev, cols_dev, count_dev, row_sources, col_tiles, True)
    grad_sum = lax.psum_scatter(
        col_terms.astype(jnp.bfloat16), "row", scatter_dimension=0, tiled=True
    ).astype(jnp.float32)
    grad_features = (inv_root * grad_sum).astype(jnp.bfloat16)
    return (hidden, grad_features, grad_weight, grad_bias)


def solution(mesh):
    placed = (
        P(("row", "col"), None),
        P(("row", "col")),
        P(),
        P(),
        P(("row", "col"), None),
        P("row", "col", None),
        P("row", "col", None),
        P("row", "col", None),
        P("row", "col", None, None),
    )
    return jax.shard_map(
        local,
        mesh=mesh,
        in_specs=placed,
        out_specs=(P(("row", "col"), None), P(("row", "col"), None), P(), P()),
        check_vma=False,
    )
```

profile of v0, /device:TPU:1, one launch (start us, length us, event | category | flops | bytes accessed | tf_op | source)
XLA Modules:
  0.0 838.9 jit_solution(7499523494927583328)
XLA Ops:
  9.6 86.1 %all-gather.3.cloned.1.call-done = bf16[8192,128]{1,0:T(8,128)(2,1)} async-done(((bf16[256,128]{1,0:T(8,128)(2,1)}), bf16[8192,128]{1,0:T(8,128)(2,1)}) %all-gather.3.cloned.1.call-update) | async-done | bytes 2097168 | tf_op jit(solution)/shard_map/all_gather | solution.py:76
  96.0 66.9 %while.30 = (s32[]{:T(128)}, f32[32,128,128]{2,1,0:T(8,128)S(1)}, s32[128]{0:T(128)S(1)}, s32[128,256]{1,0:T(8,128)}, s32[]{:T(128)}, /*index=5*/s32[128]{0:T(12...) while((s32[]{:T(128)}, f32[32,128,128]{2,1,0:T(8,128)S(1)}, ...), condition=%wide.region_2.3_spmd, body=%wide.region_0.2_spmd.sunk | while | flops 70519992 | bytes 5837511 | solution.py:42
  97.5 3.0 gather_fusion
  105.9 3.0 gather_fusion
  114.3 3.0 gather_fusion
  122.6 3.0 gather_fusion
  131.0 3.0 gather_fusion
  139.4 3.0 gather_fusion
  147.7 3.0 gather_fusion
  164.1 61.1 %reduce-scatter.3.cloned.1.call-done = bf16[256,128]{1,0:T(8,128)(2,1)} async-done(((bf16[4096,128]{1,0:T(8,128)(2,1)}), bf16[256,128]{1,0:T(8,128)(2,1)}) %reduce-scatter.3.cloned.1.call-update) | async-done | bytes 65552 | tf_op jit(solution)/shard_map/reduce_scatter | solution.py:80
  227.9 43.0 %all-gather.5.cloned.1.call-done = bf16[4096,128]{1,0:T(8,128)(2,1)} async-done(((bf16[256,128]{1,0:T(8,128)(2,1)}), bf16[4096,128]{1,0:T(8,128)(2,1)}) %all-gather.5.cloned.1.call-update) | async-done | bytes 1048592 | tf_op jit(solution)/shard_map/all_gather | solution.py:90
  273.3 64.0 %while.31 = (s32[]{:T(128)}, f32[64,128,128]{2,1,0:T(8,128)}, s32[128]{0:T(128)S(1)}, s32[128,256]{1,0:T(8,128)}, s32[]{:T(128)}, /*index=5*/s32[128]{0:T(128)S(...) while((s32[]{:T(128)}, f32[64,128,128]{2,1,0:T(8,128)}, ...), condition=%wide.region_6.7_spmd, body=%wide.region_4.6_spmd.sunk | while | flops 70519992 | bytes 5837511 | solution.py:42
  277.9 3.4 scatter_fusion.1
  285.9 3.4 scatter_fusion.1
  293.9 3.4 scatter_fusion.1
  301.9 3.3 scatter_fusion.1
  309.8 3.4 scatter_fusion.1
  317.8 3.4 scatter_fusion.1
  325.9 3.4 scatter_fusion.1
  333.9 3.4 scatter_fusion.1
  337.3 3.9 convert_element_type.62
  341.3 98.6 %psum.15 = f32[128]{0:T(128)} all-reduce(f32[128]{0:T(128)S(1)} %broadcast_multiply_fusion.2), channel_id=1, replica_groups=mesh['row'=32,'col'=16] {'row','col'}, use_global_device_ids=true, to_apply=%region_10.11 | all-reduce | flops 128 | bytes 1024 | tf_op jit(solution)/shard_map/psum | solution.py:87
  440.8 117.3 %reduce-scatter.5.cloned.1.call-done = bf16[256,128]{1,0:T(8,128)(2,1)} async-done(((bf16[8192,128]{1,0:T(8,128)(2,1)}), bf16[256,128]{1,0:T(8,128)(2,1)}) %reduce-scatter.5.cloned.1.call-update) | async-done | bytes 65552 | tf_op jit(solution)/shard_map/reduce_scatter | solution.py:93
  559.7 271.2 %all-reduce.2.cloned.1.call-done = f32[128,128]{1,0:T(8,128)} async-done(((f32[128,128]{1,0:T(8,128)}), f32[128,128]{1,0:T(8,128)}) %all-reduce.2.cloned.1.call-update) | async-done | bytes 65552 | tf_op jit(solution)/shard_map/psum | solution.py:87
  (132 shorter events, 95.1 us)
Async XLA Ops:
  7.2 218.1 %copy-start = (bf16[128,128]{1,0:T(8,128)(2,1)S(1)}, bf16[128,128]{1,0:T(8,128)(2,1)}, u32[]{:S(2)}) copy-start(bf16[128,128]{1,0:T(8,128)(2,1)} %param.15) | copy-start | bytes 98308
  7.2 88.8 %copy-start.3 = (s32[1,1,128]{2,1,0:T(1,128)S(1)}, s32[1,1,128]{2,1,0:T(1,128)}, u32[]{:S(2)}) copy-start(s32[1,1,128]{2,1,0:T(1,128)} %param.19) | copy-start | bytes 1540
  7.2 88.8 %copy-start.2 = (s32[1,1,128]{2,1,0:T(1,128)S(1)}, s32[1,1,128]{2,1,0:T(1,128)}, u32[]{:S(2)}) copy-start(s32[1,1,128]{2,1,0:T(1,128)} %param.18) | copy-start | bytes 1540
  7.2 88.5 %all-gather.3.cloned.1.call-start = ((), (), s32[]{:S(2)}) async-start(), calls=%async_computation.2 | async-start | bytes 2162688 | tf_op jit(solution)/shard_map/all_gather | solution.py:76
  9.5 215.7 %reduce-scatter.3.cloned.1.call-start = ((), (), s32[]{:S(2)}) async-start(), calls=%async_computation.3 | async-start | bytes 1114112 | tf_op jit(solution)/shard_map/reduce_scatter | solution.py:80
  162.9 62.3 %copy-start.4 = (bf16[256,128]{1,0:T(8,128)(2,1)S(1)}, bf16[256,128]{1,0:T(8,128)(2,1)}, u32[]{:S(2)}) copy-start(bf16[256,128]{1,0:T(8,128)(2,1)} %param.17) | copy-start | bytes 196612
  162.9 62.3 %copy-start.6 = (f32[128]{0:T(128)S(1)}, f32[128]{0:T(128)}, u32[]{:S(2)}) copy-start(f32[128]{0:T(128)} %param.16) | copy-start | bytes 1540
  164.1 106.8 %all-gather.5.cloned.1.call-start = ((), (), s32[]{:S(2)}) async-start(), calls=%async_computation.4 | async-start | bytes 1114112 | tf_op jit(solution)/shard_map/all_gather | solution.py:90
  227.8 330.3 %reduce-scatter.5.cloned.1.call-start = ((), (), s32[]{:S(2)}) async-start(), calls=%async_computation.5 | async-start | bytes 2162688 | tf_op jit(solution)/shard_map/reduce_scatter | solution.py:93
  270.9 2.5 copy-start.1
  341.2 98.7 %copy-start.5 = (bf16[256,128]{1,0:T(8,128)(2,1)S(1)}, bf16[256,128]{1,0:T(8,128)(2,1)}, u32[]{:S(2)}) copy-start(bf16[256,128]{1,0:T(8,128)(2,1)} %reduce-scatter.3.cloned.1.call-done) | copy-start | bytes 196612
  341.2 489.7 %all-reduce.2.cloned.1.call-start = ((), (), s32[]{:S(2)}) async-start(), calls=%async_computation.6 | async-start | bytes 131072 | tf_op jit(solution)/shard_map/psum | solution.py:87
Sparse Core Ops, SparseCore 0:
  11.8 83.9 all-gather.2
  164.2 60.9 reduce-scatter.2
  227.9 42.8 all-gather.4
  341.3 216.7 reduce-scatter.4
  563.5 267.3 all-reduce.1
where the time goes:
time: 841 us; the launch traced here: 839 us
  waiting for transfers between devices  579 us (69%)
  blocking collectives  98.6 us (12%)
  other arithmetic  73.3 us (9%)
  matrix products  40.1 us (5%)
  local copies, waits for them, and re-layouts  33.5 us (4%)
  between operations  13.9 us (2%)
    psum x1, waiting for transfers between devices, local(): lax.psum((grad_weight * grad_scale, grad_bias * grad_scale), ('row', 'col'))  271 us
    reduce_scatter x1, waiting for transfers between devices, local(): lax.psum_scatter(col_terms.astype(jnp.bfloat16), 'row', scatter_dimension...  117 us
    psum x1, blocking collectives, local(): lax.psum((grad_weight * grad_scale, grad_bias * grad_scale), ('row', 'col'))  98.6 us
    all_gather x1, waiting for transfers between devices, local(): lax.all_gather(scaled, 'row', axis=0, tiled=True)  86.1 us
    reduce_scatter x1, waiting for transfers between devices, local(): lax.psum_scatter(row_terms.astype(jnp.bfloat16), 'col', scatter_dimension...  61.1 us
    all_gather x1, waiting for transfers between devices, local(): row_grads = lax.all_gather(grad_scaled, 'col', axis=0, tiled=True)  43 us
    scatter-add x16, other arithmetic, block_step(): return summed.at[target].add(product)  39.9 us
    gather x16, local copies, waits for them, and re-layouts, block_step(): picked = jnp.take(source, anchor, axis=0)  29.3 us
  transfers between devices with their start and end apart: 5, of which 5 were waited for; matrix products, arithmetic and copies ran while one was open for 0% of the time, Pallas kernels for 0%

commit v1 on v0

v1 whole, which is shorter than its diff:
```python
import functools
import math

import jax
import jax.numpy as jnp
from jax import lax
from jax.experimental import pallas as pl
from jax.experimental.pallas import tpu as pltpu
from jax.sharding import PartitionSpec as P

MESH = pl.DeviceIdType.MESH
F32 = jnp.float32
BF16 = jnp.bfloat16
I32 = jnp.int32

NX, NY, NZ = 4, 8, 8
PIECE = 256
T = 128
SLOTS = 128
PRIME = 4093
ROUND = 12582912.0
CUT = 96

WIRE = 46e3
CORE_WIRE = 250e3
HOP = 1.7
CORE_HOP = 0.95


class Plan:
    def __init__(self):
        self.copies = {}
        self.actions = []
        self.fillers = []

    def message(self, key, link, nbytes, make):
        self.copies[key] = [link, nbytes, make, None]

    def action(self, deps, fn, sends=(), cost=0.03):
        self.actions.append((tuple(deps), fn, tuple(sends), cost))

    def filler(self, fn, cost):
        self.fillers.append((fn, cost))

    def run(self, leave=()):
        now = 0.0
        free = {}
        arrival = {}
        todo = list(self.actions)
        fill = list(self.fillers)
        waited = set()
        while todo:
            best, best_at = None, None
            for item in todo:
                if all(d in arrival for d in item[0]):
                    at = max([now] + [arrival[d] for d in item[0]])
                    if best is None or at < best_at - 1e-9:
                        best, best_at = item, at
            if fill and best_at > now + 0.1:
                fn, cost = fill.pop(0)
                fn()
                now += cost
                continue
            deps, fn, sends, cost = best
            todo.remove(best)
            for d in sorted(deps, key=lambda d: arrival[d]):
                if d not in waited:
                    waited.add(d)
                    self.copies[d][3].wait_recv()
            now = best_at
            if fn is not None:
                fn()
                now += cost
            for key in sends:
                link, nbytes, make, _ = self.copies[key]
                copy = make()
                self.copies[key][3] = copy
                copy.start()
                wire, hop = (CORE_WIRE, CORE_HOP) if link[0] == "c" else (WIRE, HOP)
                free[link] = max(free.get(link, 0.0), now) + nbytes / wire
                arrival[key] = free[link] + hop
        for fn, cost in fill:
            fn()
        for key, item in self.copies.items():
            if key not in waited and key not in leave:
                item[3].wait_recv()

    def drain(self):
        for item in self.copies.values():
            item[3].wait_send()


class Place:
    def __init__(self, send_sem, recv_sem):
        self.row = row = lax.axis_index("row")
        self.col = col = lax.axis_index("col")
        self.mx, self.my = row // NY, row % NY
        self.mz, self.core = col // 2, col % 2
        self.other = (row, self.mz * 2 + (1 - self.core))
        self.send_sem, self.recv_sem = send_sem, recv_sem
        self.used = 0

    def xy_piece(self, x, y):
        return lax.rem(self.mx + x + NX, NX) * NY + lax.rem(self.my + y + NY, NY)

    def z_piece(self, z, k):
        return lax.rem(self.mz + z + NZ, NZ) * 2 + k

    def at_xy(self, x, y):
        return (self.xy_piece(x, y), self.col)

    def at_z(self, z):
        return (self.row, self.z_piece(z, self.core))

    def copier(self, src, dst, dev):
        i = self.used
        self.used += 1

        def make():
            return pltpu.make_async_remote_copy(
                src_ref=src(), dst_ref=dst(), send_sem=self.send_sem.at[i], recv_sem=self.recv_sem.at[i],
                device_id=dev, device_id_type=MESH,
            )

        return make

    def enter(self, peers):
        barrier = pltpu.get_barrier_semaphore()
        for dev in peers:
            pl.semaphore_signal(barrier, inc=1, device_id=dev, device_id_type=MESH)

        def met():
            pl.semaphore_wait(barrier, len(peers))

        return met


def rows_of(start, first, size):
    return pl.ds(pl.multiple_of(start * PIECE + first, 16), size)


def tile_rows(t):
    return pl.ds(pl.multiple_of(t * T, T), T)


def slots_of(i, n):
    return pl.ds(pl.multiple_of(i * n, 8), n)


PARTS = {"A": (0, CUT), "B": (CUT, PIECE - CUT)}


def half(first, size, d):
    return (first, size // 2) if d > 0 else (first + size // 2, size // 2)


def part_rows(which, d, last):
    first, size = PARTS[which]
    return half(first, size, d) if last else (first, size)


def combine(dst, src, piece, first, size, given):
    whole = all(n >= size for _, _, _, n in given)
    blocks = [(first, size)] if whole else [half(first, size, 1), half(first, size, -1)]
    for f, n in blocks:
        v = src[rows_of(piece, f, n), :].astype(F32)
        for ref, base, gf, gn in given:
            if gf <= f and f + n <= gf + gn:
                v = v + ref[pl.ds(base + f - gf, n), :].astype(F32)
        dst[rows_of(piece, f, n), :] = v.astype(BF16)


def around(n):
    out = [n // 2]
    for k in range(n // 2 - 1, 0, -1):
        out += [k, -k]
    return out + [0]


COPIES1 = 76


def gather_body(
    feat_ref, deg_ref, rows_ref, cols_ref, count_ref, codes_ref,
    xg_ref, masks_ref, tab_ref,
    at_ref, b_ref, send_sem, recv_sem,
):
    me = Place(send_sem, recv_sem)
    met = me.enter([me.at_xy(1, 0), me.at_xy(-1, 0), me.at_xy(0, 1), me.at_xy(0, -1)])
    root = lax.rsqrt(deg_ref[...].astype(F32))
    for h in range(2):
        spread = jnp.broadcast_to(root[h : h + 1, :], (T, T)).T
        xg_ref[rows_of(me.row, h * T, T), :] = (spread * feat_ref[h * T : (h + 1) * T, :].astype(F32)).astype(BF16)
    met()
    plan = Plan()

    def leg(which, axis, o, d, k):
        n = NX if axis == "x" else NY
        first, size = part_rows(which, d, k == n // 2)
        back = -d * (k - 1)
        piece = me.xy_piece(back, o) if axis == "x" else me.xy_piece(o, back)
        where = lambda: xg_ref.at[rows_of(piece, first, size), :]
        dev = me.at_xy(d, 0) if axis == "x" else me.at_xy(0, d)
        key = (which, axis, o, d, k)
        plan.message(key, (axis, d), size * 256, me.copier(where, where, dev))
        return key

    for which, one, two in (("A", "x", "y"), ("B", "y", "x")):
        n1 = NX if one == "x" else NY
        n2 = NX if two == "x" else NY
        legs = {}
        for d in (1, -1):
            for k in range(1, n1 // 2 + 1):
                legs[d, k] = leg(which, one, 0, d, k)
        for d in (1, -1):
            plan.action([], None, [legs[d, 1]])
            for k in range(2, n1 // 2 + 1):
                plan.action([legs[d, k - 1]], None, [legs[d, k]])
        for o in range(-(n1 // 2) + 1, n1 // 2 + 1):
            if o == 0:
                need = []
            elif o == n1 // 2:
                need = [legs[1, o], legs[-1, o]]
            else:
                need = [legs[-1 if o > 0 else 1, abs(o)]]
            for d in (1, -1):
                before = need
                for k in range(1, n2 // 2 + 1):
                    key = leg(which, two, o, d, k)
                    plan.action(before, None, [key])
                    before = [key]

    def tables():
        lane = lax.broadcasted_iota(I32, (T, T), 1)
        sub = lax.broadcasted_iota(I32, (T, T), 0)
        out = []
        spread = [jnp.broadcast_to(v, (T, T)) for v in (rows_ref[...], cols_ref[...])]
        stood = [v.T for v in spread]
        for mine in (0, 1):
            key_l = spread[mine] * SLOTS + lane
            key_s = stood[mine] * SLOTS + sub
            rank = jnp.sum((key_s < key_l).astype(I32), axis=0, keepdims=True)
            hot = jnp.broadcast_to(rank, (T, T)).T == lane
            pick = lambda v: jnp.sum(jnp.where(hot, v, 0), axis=0, keepdims=True)
            order = pick(sub)
            target = pick(stood[mine])
            source = pick(stood[1 - mine])
            same = (target == pltpu.roll(target, 1, 1)) & (lane[:1] > 0)
            last = jnp.sum((stood[mine] <= lane).astype(I32), axis=0, keepdims=True) - 1
            has = jnp.sum((stood[mine] == lane).astype(I32), axis=0, keepdims=True)
            out += [order, source, same.astype(I32), jnp.maximum(last, 0), (has > 0).astype(I32)]
        for i, v in enumerate(out):
            tab_ref[i : i + 1, :] = v

    def codes_ready():
        live = lax.broadcasted_iota(I32, (SLOTS, T), 0) < count_ref[0, 0]
        a = codes_ref[:, :T] + 3
        a = jnp.where(a >= PRIME, a - PRIME, a)
        a = jnp.where(live, a, 0)
        at_ref[...] = a.astype(F32).T
        b = codes_ref[:, T:] + 1
        b_ref[...] = jnp.where(b >= PRIME, b - PRIME, b).astype(F32)

    def mask_group(g):
        at = at_ref[...]
        for u in range(8):
            s = g * 8 + u
            prod = at[:, u : u + 1] * b_ref[s : s + 1, :]
            near_q = (prod * (1.0 / PRIME) + ROUND) - ROUND
            left = prod - near_q * PRIME
            hit = (left >= 3.0) & (left < 67.0)
            masks_ref[s * T : (s + 1) * T, :] = jnp.where(hit, 1.0, 0.0).astype(BF16)
        at_ref[...] = pltpu.roll(at, T - 8, 1)

    plan.filler(codes_ready, 0.3)
    for g in range(SLOTS // 8):
        plan.filler(functools.partial(mask_group, g), 0.35)
    plan.filler(tables, 0.8)
    plan.run()
    plan.drain()


UNROLL = 8


def product_body(forward, tiles, tab_ref, masks_ref, src_ref, out_ref, pre_ref):
    base = 0 if forward else 5

    def step(g, acc):
        for u in range(UNROLL):
            j = g * UNROLL + u
            mask = masks_ref[tile_rows(tab_ref[base, j]), :]
            src = src_ref[tile_rows(tab_ref[base + 1, j]), :]
            new = jnp.dot(mask, src, preferred_element_type=F32) if forward else jnp.dot(src, mask, preferred_element_type=F32)
            acc = acc * tab_ref[base + 2, j].astype(F32) + new
            pre_ref[tile_rows(j), :] = acc
        return acc

    lax.fori_loop(0, SLOTS // UNROLL, step, jnp.zeros((T, T), F32))
    for t in range(tiles):
        v = pre_ref[tile_rows(tab_ref[base + 3, t]), :]
        out_ref[t * T : (t + 1) * T, :] = (v * tab_ref[base + 4, t].astype(F32)).astype(BF16)


COPIES2 = 40
W1 = T // 2
WZ = W1 // NZ


def dense_body(
    rp_ref, deg_ref, weight_ref, bias_ref, cot_ref,
    hid_ref, gt_ref, gsum_ref,
    acc_ref, cs_ref, zs_ref, gl_ref, g1_ref, gz_ref, g2_ref, send_sem, recv_sem,
):
    me = Place(send_sem, recv_sem)
    core, mz = me.core, me.mz
    met = me.enter([me.other] + [me.at_z(o) for o in range(1, NZ)])
    root = lax.rsqrt(deg_ref[...].astype(F32))
    met()
    plan = Plan()
    offsets = around(NZ)
    for i, o in enumerate(offsets):
        plan.message(
            ("c", o), ("c", 1), 65536,
            me.copier(
                functools.partial(lambda p: rp_ref.at[rows_of(p, 0, PIECE), :], me.z_piece(o, 1 - core)),
                functools.partial(lambda i: cs_ref.at[pl.ds(i * PIECE, PIECE), :], i),
                me.other,
            ),
        )
        plan.action([], None, [("c", o)], 0.05)
    legs = {}
    base = 0
    for d in (1, -1):
        for k in range(NZ // 2, 0, -1):
            first, size = (0, PIECE) if k < NZ // 2 else half(0, PIECE, d)
            piece = me.z_piece(d * k, core)
            legs[d, k] = (base, first, size, piece)
            plan.message(
                ("z", d, k), ("z", d), size * 256,
                me.copier(
                    functools.partial(lambda p, f, s: acc_ref.at[rows_of(p, f, s), :], piece, first, size),
                    functools.partial(lambda b, s: zs_ref.at[pl.ds(b, s), :], base, size),
                    me.at_z(d),
                ),
            )
            base += size

    def z_add(d, k):
        o = NZ // 2 if k == NZ // 2 else d * k
        _, first, size, piece = legs[d, k]
        given = [(cs_ref, offsets.index(o) * PIECE + first, first, size)]
        if k < NZ // 2:
            b, f, n, _ = legs[d, k + 1]
            given.append((zs_ref, b, f, n))
        combine(acc_ref, rp_ref, piece, first, size, given)

    for k in range(NZ // 2, 0, -1):
        for d in (1, -1):
            deps = [("c", NZ // 2 if k == NZ // 2 else d * k)]
            if k < NZ // 2:
                deps.append(("z", d, k + 1))
            plan.action(deps, functools.partial(z_add, d, k), [("z", d, k)], 0.08)
    plan.run()

    i0 = offsets.index(0)
    agg_sum = rp_ref[rows_of(me.col, 0, PIECE), :].astype(F32) + cs_ref[i0 * PIECE : (i0 + 1) * PIECE, :].astype(F32)
    for d in (1, -1):
        b = legs[d, 1][0]
        agg_sum = agg_sum + zs_ref[b : b + PIECE, :].astype(F32)
    spread = jnp.concatenate([jnp.broadcast_to(root[h : h + 1, :], (T, T)).T for h in range(2)], axis=0)
    aggregate = (spread * agg_sum).astype(BF16)
    weight = weight_ref[...]
    preact = jnp.dot(aggregate, weight, preferred_element_type=F32) + bias_ref[...]
    below = jnp.exp(jnp.minimum(preact, 0.0))
    hid_ref[...] = jnp.where(preact > 0, preact, below - 1.0).astype(BF16)
    grad_pre = cot_ref[...].astype(F32) * jnp.where(preact > 0, 1.0, below)
    grad_pre_b = grad_pre.astype(BF16)
    grad_agg_t = lax.dot_general(weight, grad_pre_b, (((1,), (1,)), ((), ())), preferred_element_type=F32)
    for h in range(2):
        gt_ref[rows_of(me.col, h * T, T), :] = (grad_agg_t[:, h * T : (h + 1) * T] * root[h : h + 1, :]).astype(BF16)

    plan2 = Plan()
    for d in (1, -1):
        for k in range(1, NZ // 2 + 1):
            first, size = (0, PIECE) if k < NZ // 2 else half(0, PIECE, d)
            piece = me.z_piece(-d * (k - 1), core)
            where = functools.partial(lambda p, f, s: gt_ref.at[rows_of(p, f, s), :], piece, first, size)
            plan2.message(("Z", d, k), ("z", d), size * 256, me.copier(where, where, me.at_z(d)))
    for o in offsets:
        where = functools.partial(lambda p: gt_ref.at[rows_of(p, 0, PIECE), :], me.z_piece(o, core))
        plan2.message(("C", o), ("c", 1), 65536, me.copier(where, where, me.other))
    plan2.action([], None, [("Z", 1, 1), ("Z", -1, 1), ("C", 0)])
    for d in (1, -1):
        for k in range(2, NZ // 2 + 1):
            plan2.action([("Z", d, k - 1)], None, [("Z", d, k)])
    for k in range(1, NZ // 2 + 1):
        if k == NZ // 2:
            plan2.action([("Z", 1, k), ("Z", -1, k)], None, [("C", k)])
        else:
            for d in (1, -1):
                plan2.action([("Z", d, k)], None, [("C", -d * k)])

    scale = 1.0 / math.sqrt(PIECE * NX * NY * NZ * 2)

    def grads():
        agg_t = aggregate.astype(F32).T.astype(BF16)
        gw = jnp.dot(agg_t, grad_pre_b, preferred_element_type=F32) * scale
        gb = jnp.sum(grad_pre, axis=0, keepdims=True) * scale
        gb8 = jnp.where(lax.broadcasted_iota(I32, (8, T), 0) == 0, gb, 0.0)
        for k in range(2):
            gl_ref[k * 72 : k * 72 + W1, :] = gw[k * W1 : (k + 1) * W1, :]
            gl_ref[k * 72 + W1 : (k + 1) * 72, :] = gb8

    plan2.message(
        ("G", 1), ("c", 1), 72 * 512,
        me.copier(lambda: gl_ref.at[slots_of(1 - core, 72), :], lambda: g1_ref.at[:, :], me.other),
    )
    plan2.action([], grads, [("G", 1)], 0.5)
    g2 = []
    for o in range(1, NZ):
        g2.append(("G2", o))
        plan2.message(
            ("G2", o), ("gz", o), 16 * 512,
            me.copier(
                functools.partial(lambda o: gz_ref.at[slots_of(lax.rem(mz + o, NZ), 16), :], o),
                lambda: g2_ref.at[slots_of(mz, 16), :],
                me.at_z(o),
            ),
        )

    def after_chip():
        total = gl_ref[slots_of(core, 72), :] + g1_ref[...]
        for z in range(NZ):
            gz_ref[z * 16 : z * 16 + 8, :] = total[z * WZ : (z + 1) * WZ, :]
            gz_ref[z * 16 + 8 : z * 16 + 16, :] = total[W1 : W1 + 8, :]
        g2_ref[slots_of(mz, 16), :] = gz_ref[slots_of(mz, 16), :]

    plan2.action([("G", 1)], after_chip, g2, 0.2)

    def after_z():
        gsum_ref[...] = total_of(g2_ref, NZ)

    plan2.action(g2, after_z, (), 0.1)
    plan2.run()
    plan.drain()
    plan2.drain()


def total_of(ref, n):
    v = ref[0:16, :]
    for i in range(1, n):
        v = v + ref[i * 16 : (i + 1) * 16, :]
    return v


COPIES3 = 76 + 3 + 7 + 7 + 1


def scatter_body(
    cp_ref, deg_ref, gsum_ref,
    gf_ref, gw_ref, gb_ref,
    acc_ref, sum_ref, g3_ref, g3x_ref, g4_ref, yx_ref, send_sem, recv_sem,
):
    me = Place(send_sem, recv_sem)
    core, mz, mx, my = me.core, me.mz, me.mx, me.my
    met = me.enter(
        [me.other]
        + [me.at_z(o) for o in range(1, NZ)]
        + [me.at_xy(o, 0) for o in range(1, NX)]
        + [me.at_xy(0, o) for o in range(1, NY)]
    )
    root = lax.rsqrt(deg_ref[...].astype(F32))
    met()
    plan = Plan()
    slot_rows = [0]

    def leg(which, axis, o, d, k, src):
        n = NX if axis == "x" else NY
        first, size = part_rows(which, d, k == n // 2)
        piece = me.xy_piece(d * k, o) if axis == "x" else me.xy_piece(o, d * k)
        base = slot_rows[0]
        slot_rows[0] += size
        dev = me.at_xy(d, 0) if axis == "x" else me.at_xy(0, d)
        key = ("s", which, axis, o, d, k)
        plan.message(
            key, (axis, d), size * 256,
            me.copier(
                lambda: src.at[rows_of(piece, first, size), :], lambda: sum_ref.at[pl.ds(base, size), :], dev
            ),
        )
        return dict(key=key, base=base, first=first, size=size, piece=piece)

    def given(*legs):
        return [(sum_ref, e["base"], e["first"], e["size"]) for e in legs]

    def adder(leg, *others):
        return lambda: combine(acc_ref, cp_ref, leg["piece"], leg["first"], leg["size"], given(*others))

    finals = {}
    late = []
    for which, one, two in (("A", "y", "x"), ("B", "x", "y")):
        n1 = NX if one == "x" else NY
        n2 = NX if two == "x" else NY
        done = {}
        for o in around(n2):
            ends = []
            for d in (1, -1):
                prev = None
                for k in range(n1 // 2, 0, -1):
                    now = leg(which, one, o, d, k, cp_ref if prev is None else acc_ref)
                    if prev is None:
                        plan.action([], None, [now["key"]])
                    else:
                        late.append(([prev["key"]], adder(now, prev), [now["key"]], 0.05))
                    prev = now
                ends.append(prev)
            done[o] = ends
        legs = {}
        for d in (1, -1):
            for k in range(n2 // 2, 0, -1):
                now = legs[d, k] = leg(which, two, 0, d, k, acc_ref)
                more = done[n2 // 2 if k == n2 // 2 else d * k] + ([legs[d, k + 1]] if k < n2 // 2 else [])
                late.append(([e["key"] for e in more], adder(now, *more), [now["key"]], 0.08))
        finals[which] = done[0] + [legs[1, 1], legs[-1, 1]]
    for deps, fn, sends, cost in late:
        plan.action(deps, fn, sends, cost)

    def ride(tag, n, dev, where, size):
        keys = []
        for o in range(1, n):
            keys.append((tag, o))
            plan.message((tag, o), (tag, o), size * 512, me.copier(where, where, dev(o)))
        return keys

    g3x = ride("G3x", NX, lambda o: me.at_xy(o, 0), lambda: g3x_ref.at[slots_of(mx, 16), :], 16)

    def start_x():
        g3x_ref[slots_of(mx, 16), :] = gsum_ref[...]

    plan.action([], start_x, g3x, 0.02)
    g3y = ride("G3y", NY, lambda o: me.at_xy(0, o), lambda: g3_ref.at[slots_of(my, 16), :], 16)

    def after_x():
        g3_ref[slots_of(my, 16), :] = total_of(g3x_ref, NX)

    plan.action(g3x, after_x, g3y, 0.05)
    own_w = lambda: pl.ds(pl.multiple_of(core * W1 + mz * WZ, 8), WZ)
    g4 = ride("G4", NZ, me.at_z, lambda: g4_ref.at[own_w(), :], WZ)

    def after_y():
        v = total_of(g3_ref, NY)
        gb_ref[...] = v[8:9, :]
        g4_ref[own_w(), :] = v[0:8, :]

    plan.action(g3y, after_y, g4, 0.05)
    half_w = lambda: g4_ref.at[slots_of(core, W1), :]
    plan.message(("G5", 0), ("c", 1), W1 * 512, me.copier(half_w, half_w, me.other))
    plan.action(g4, None, [("G5", 0)])

    def give_weight():
        gw_ref[...] = g4_ref[...]

    plan.action([("G5", 0)], give_weight, (), 0.05)
    plan.run()

    for which in ("A", "B"):
        first, size = PARTS[which]
        v = cp_ref[rows_of(me.row, first, size), :].astype(F32)
        for e in finals[which]:
            v = v + sum_ref[pl.ds(e["base"], e["size"]), :].astype(F32)
        yx_ref[first : first + size, :] = v
    for h in range(2):
        v = yx_ref[h * T : (h + 1) * T, :] * root[h : h + 1, :]
        gf_ref[h * T : (h + 1) * T, :] = v.T.astype(BF16)
    plan.drain()


VMEM = pl.BlockSpec(memory_space=pltpu.VMEM)
SMEM = pl.BlockSpec(memory_space=pltpu.SMEM)
ROW_NODES = PIECE * NZ * 2
COL_NODES = PIECE * NX * NY


def call(body, outs, ins, scratch, name, **params):
    return pl.pallas_call(
        body,
        out_shape=tuple(jax.ShapeDtypeStruct(*o) for o in outs),
        in_specs=ins,
        out_specs=(VMEM,) * len(outs),
        scratch_shapes=scratch,
        compiler_params=pltpu.CompilerParams(**params),
        name=name,
    )


def sems(n):
    return [pltpu.SemaphoreType.DMA((n,)), pltpu.SemaphoreType.DMA((n,))]


def local(features, degree, weight, bias, cotangent, tile_rows, tile_cols, tile_count, tile_codes):
    degree = degree.reshape(2, T)
    gather = call(
        gather_body,
        [((COL_NODES, T), BF16), ((SLOTS * T, T), BF16), ((16, T), I32)],
        [VMEM] * 4 + [SMEM, VMEM],
        [pltpu.VMEM((T, SLOTS), F32), pltpu.VMEM((SLOTS, T), F32)] + sems(COPIES1),
        "gather", collective_id=0, has_side_effects=True,
    )
    gathered, masks, table = gather(
        features, degree, tile_rows.reshape(1, SLOTS), tile_cols.reshape(1, SLOTS),
        tile_count.reshape(1, 1), tile_codes.reshape(SLOTS, 2 * T),
    )
    forward = call(
        functools.partial(product_body, True, ROW_NODES // T),
        [((ROW_NODES, T), BF16)],
        [SMEM, VMEM, VMEM],
        [pltpu.VMEM((SLOTS * T, T), F32)],
        "forward",
    )
    (row_terms,) = forward(table, masks, gathered)
    dense = call(
        dense_body,
        [((PIECE, T), BF16), ((ROW_NODES, T), BF16), ((16, T), F32)],
        [VMEM] * 5,
        [
            pltpu.VMEM((ROW_NODES, T), BF16),
            pltpu.VMEM((PIECE * NZ, T), BF16),
            pltpu.VMEM((PIECE * (NZ - 1), T), BF16),
            pltpu.VMEM((144, T), F32),
            pltpu.VMEM((72, T), F32),
            pltpu.VMEM((16 * NZ, T), F32),
            pltpu.VMEM((16 * NZ, T), F32),
        ]
        + sems(COPIES2),
        "dense", collective_id=1, has_side_effects=True,
    )
    hidden, grads_t, gsum = dense(row_terms, degree, weight, bias.reshape(1, T), cotangent)
    backward = call(
        functools.partial(product_body, False, COL_NODES // T),
        [((COL_NODES, T), BF16)],
        [SMEM, VMEM, VMEM],
        [pltpu.VMEM((SLOTS * T, T), F32)],
        "backward",
    )
    (col_terms,) = backward(table, masks, grads_t)
    scatter = call(
        scatter_body,
        [((PIECE, T), BF16), ((T, T), F32), ((1, T), F32)],
        [VMEM] * 3,
        [
            pltpu.VMEM((COL_NODES, T), BF16),
            pltpu.VMEM((COL_NODES - PIECE, T), BF16),
            pltpu.VMEM((16 * NY, T), F32),
            pltpu.VMEM((16 * NX, T), F32),
            pltpu.VMEM((T, T), F32),
            pltpu.VMEM((PIECE, T), F32),
        ]
        + sems(COPIES3),
        "scatter", collective_id=2, has_side_effects=True,
    )
    grad_features, grad_weight, grad_bias = scatter(col_terms, degree, gsum)
    return hidden, grad_features, grad_weight, grad_bias.reshape(T)


def solution(mesh):
    placed = (
        P(("row", "col"), None),
        P(("row", "col")),
        P(),
        P(),
        P(("row", "col"), None),
        P("row", "col", None),
        P("row", "col", None),
        P("row", "col", None),
        P("row", "col", None, None),
    )
    return jax.shard_map(
        local,
        mesh=mesh,
        in_specs=placed,
        out_specs=(P(("row", "col"), None), P(("row", "col"), None), P(), P()),
        check_vma=False,
    )
```

time: 841 us -> 137 us (0.16)
  waiting for transfers between devices: 579 us -> 0 us
  Pallas kernels: 0 us -> 129 us
  blocking collectives: 98.6 us -> 0 us
  other arithmetic: 73.3 us -> 0 us
  matrix products: 40.1 us -> 0 us
  local copies, waits for them, and re-layouts: 33.5 us -> 4.71 us
  between operations: 13.9 us -> 1.31 us
    psum x1 -> x0, waiting for transfers between devices: 271 us -> none  [local(): lax.psum((grad_weight * grad_scale, grad_bias * grad_scale), ('row', 'col'))]
    reduce_scatter x2 -> x0, waiting for transfers between devices: 178 us -> none  [the longest x1 117 us: local(): lax.psum_scatter(col_terms.astype(jnp.bfloat16), 'row', scatter_dimension...]
    all_gather x2 -> x0, waiting for transfers between devices: 129 us -> none  [the longest x1 86.1 us: local(): lax.all_gather(scaled, 'row', axis=0, tiled=True)]
    pallas_call x0 -> x5, Pallas kernels: none -> 129 us  [the longest x1 47.5 us: local(): dense(row_terms, degree, weight, bias.reshape(1, T), cotangent)]
    psum x1 -> x0, blocking collectives: 98.6 us -> none  [local(): lax.psum((grad_weight * grad_scale, grad_bias * grad_scale), ('row', 'col'))]
    dot_general x19 -> x0, matrix products: 40.1 us -> none  [the longest x8 19.3 us: block_step(): jnp.einsum('tij,tif->tjf', keep, picked, preferred_element_type=jnp.float32)]
    scatter-add x16 -> x0, other arithmetic: 39.9 us -> none  [block_step(): return summed.at[target].add(product)]
    gather x16 -> x0, local copies, waits for them, and re-layouts: 29.3 us -> none  [block_step(): picked = jnp.take(source, anchor, axis=0)]
  transfers between devices with their start and end apart: 5 -> 0, of which waited for: 5 -> 0; matrix products, arithmetic and copies ran while one was open for 0% -> 0% of each run, Pallas kernels for 0% -> 0%
where the time goes in v1:
time: 137 us; the launch traced here: 135 us
  Pallas kernels  129 us (94%)
  local copies, waits for them, and re-layouts  4.71 us (3%)
    pallas_call x1, Pallas kernels, local(): dense(row_terms, degree, weight, bias.reshape(1, T), cotangent)  47.5 us
    pallas_call x1, Pallas kernels, local(): grad_features, grad_weight, grad_bias = scatter(col_terms, degree, gsum)  37.2 us
    pallas_call x1, Pallas kernels, local(): gather(features, degree, tile_rows.reshape(1, SLOTS), tile_cols.reshape(1...  28.7 us
    pallas_call x1, Pallas kernels, local(): col_terms, = backward(table, masks, grads_t)  7.6 us
    pallas_call x1, Pallas kernels, local(): row_terms, = forward(table, masks, gathered)  7.52 us
    unnamed x6, local copies, waits for them, and re-layouts  4.71 us

profile of v1, /device:TPU:1, one launch (start us, length us, event | category | flops | bytes accessed | tf_op | source)
XLA Modules:
  0.0 134.6 jit_solution(1852283174379024341)
XLA Ops:
  1.3 28.7 %gather.1 = (bf16[8192,128]{1,0:T(8,128)(2,1)}, bf16[16384,128]{1,0:T(8,128)(2,1)}, s32[16,128]{1,0:T(8,128)}) custom-call(bf16[256,128]{1,0:T(8,128)(2,1)} %feat_ref.1, s32[2,128]{1,0:T(2,128)} %bitcast.9, s32[1,128]{1,0:T(1,128)} %bitcast.13, s32[1,128]{1,0:T(1,128)} %bitcast.14, s32[1,1]{1,0:T(1,128)} %bitcast.7.count_ref, s32[128,256]{1,0:T(8,128)} %bitcast.8), custom_call_target="tpu_custom_call" | custom-call | tf_op jit(solution)/shard_map/gather/pallas_call | solution.py:610
  30.0 7.5 %forward.1.rp_ref = bf16[4096,128]{1,0:T(8,128)(2,1)} custom-call(s32[16,128]{1,0:T(8,128)} %get-tuple-element.13.tab_ref, bf16[16384,128]{1,0:T(8,128)(2,1)} %get-tuple-element.14.masks_ref, bf16[8192,128]{1,0:T(8,128)(2,1)} %get-tuple-element.15.src_ref), custom_call_target="tpu_custom_call" | custom-call | tf_op jit(solution)/shard_map/forward/pallas_call | solution.py:621
  37.5 47.5 %dense.1 = (bf16[256,128]{1,0:T(8,128)(2,1)}, bf16[4096,128]{1,0:T(8,128)(2,1)}, f32[16,128]{1,0:T(8,128)}) custom-call(bf16[4096,128]{1,0:T(8,128)(2,1)} %forward.1.rp_ref, s32[2,128]{1,0:T(2,128)} %bitcast.10, bf16[128,128]{1,0:T(8,128)(2,1)} %weight_ref.1, f32[1,128]{1,0:T(1,128)} %bitcast.12, bf16[256,128]{1,0:T(8,128)(2,1)} %cot_ref.1), custom_call_target="tpu_custom_call" | custom-call | tf_op jit(solution)/shard_map/dense/pallas_call | solution.py:638
  85.0 7.6 %backward.1.cp_ref = bf16[8192,128]{1,0:T(8,128)(2,1)} custom-call(s32[16,128]{1,0:T(8,128)} %get-tuple-element.13.tab_ref, bf16[16384,128]{1,0:T(8,128)(2,1)} %get-tuple-element.14.masks_ref, bf16[4096,128]{1,0:T(8,128)(2,1)} %get-tuple-element.17.src_ref), custom_call_target="tpu_custom_call" | custom-call | tf_op jit(solution)/shard_map/backward/pallas_call | solution.py:646
  92.6 0.0 copy-start
  92.6 37.2 %scatter.1 = (bf16[256,128]{1,0:T(8,128)(2,1)}, f32[128,128]{1,0:T(8,128)}, f32[1,128]{1,0:T(1,128)}) custom-call(bf16[8192,128]{1,0:T(8,128)(2,1)} %backward.1.cp_ref, s32[2,128]{1,0:T(2,128)} %bitcast.11, f32[16,128]{1,0:T(8,128)} %get-tuple-element.18.gsum_ref), custom_call_target="tpu_custom_call" | custom-call | tf_op jit(solution)/shard_map/scatter/pallas_call | solution.py:662
  129.9 0.0 copy-done
  129.9 0.6 copy.18
  130.5 1.5 %copy.19 = bf16[256,128]{1,0:T(8,128)(2,1)} copy(bf16[256,128]{1,0:T(8,128)(2,1)} %get-tuple-element.27) | data formatting | bytes 131072
  132.0 1.5 %copy.20 = f32[128,128]{1,0:T(8,128)} copy(f32[128,128]{1,0:T(8,128)} %get-tuple-element.28) | data formatting | bytes 131072
  133.5 1.1 copy.21
Async XLA Ops:
  92.6 37.2 %copy-start = (bf16[256,128]{1,0:T(8,128)(2,1)S(1)}, bf16[256,128]{1,0:T(8,128)(2,1)}, u32[]{:S(2)}) copy-start(bf16[256,128]{1,0:T(8,128)(2,1)} %get-tuple-element.26) | copy-start | bytes 196612

commit v2 on v1

--- a/solution.py
+++ b/solution.py
@@ -177,17 +177,7 @@
     return out + [0]
 
 
-COPIES1 = 76
-
-
-def gather_body(
-    feat_ref, deg_ref, rows_ref, cols_ref, count_ref, codes_ref,
-    xg_ref, masks_ref, tab_ref,
-    at_ref, b_ref, send_sem, recv_sem,
-):
-    me = Place(send_sem, recv_sem)
-    met = me.enter([me.at_xy(1, 0), me.at_xy(-1, 0), me.at_xy(0, 1), me.at_xy(0, -1)])
-    root = lax.rsqrt(deg_ref[...].astype(F32))
+def gather_part(me, root, met, feat_ref, rows_ref, cols_ref, count_ref, codes_ref, xg_ref, masks_ref, tab_ref, at_ref, b_ref):
     for h in range(2):
         spread = jnp.broadcast_to(root[h : h + 1, :], (T, T)).T
         xg_ref[rows_of(me.row, h * T, T), :] = (spread * feat_ref[h * T : (h + 1) * T, :].astype(F32)).astype(BF16)
@@ -277,20 +267,24 @@
         plan.filler(functools.partial(mask_group, g), 0.35)
     plan.filler(tables, 0.8)
     plan.run()
-    plan.drain()
+    return [plan]
 
 
 UNROLL = 8
 
 
-def product_body(forward, tiles, tab_ref, masks_ref, src_ref, out_ref, pre_ref):
+def tile_at(t):
+    return pl.ds(t * T, T)
+
+
+def product_part(forward, tiles, tab_ref, masks_ref, src_ref, out_ref, pre_ref):
     base = 0 if forward else 5
 
     def step(g, acc):
         for u in range(UNROLL):
             j = g * UNROLL + u
-            mask = masks_ref[tile_rows(tab_ref[base, j]), :]
-            src = src_ref[tile_rows(tab_ref[base + 1, j]), :]
+            mask = masks_ref[tile_at(tab_ref[base, j]), :]
+            src = src_ref[tile_at(tab_ref[base + 1, j]), :]
             new = jnp.dot(mask, src, preferred_element_type=F32) if forward else jnp.dot(src, mask, preferred_element_type=F32)
             acc = acc * tab_ref[base + 2, j].astype(F32) + new
             pre_ref[tile_rows(j), :] = acc
@@ -298,25 +292,19 @@
 
     lax.fori_loop(0, SLOTS // UNROLL, step, jnp.zeros((T, T), F32))
     for t in range(tiles):
-        v = pre_ref[tile_rows(tab_ref[base + 3, t]), :]
+        v = pre_ref[tile_at(tab_ref[base + 3, t]), :]
         out_ref[t * T : (t + 1) * T, :] = (v * tab_ref[base + 4, t].astype(F32)).astype(BF16)
 
 
-COPIES2 = 40
 W1 = T // 2
 WZ = W1 // NZ
 
 
-def dense_body(
-    rp_ref, deg_ref, weight_ref, bias_ref, cot_ref,
-    hid_ref, gt_ref, gsum_ref,
-    acc_ref, cs_ref, zs_ref, gl_ref, g1_ref, gz_ref, g2_ref, send_sem, recv_sem,
+def dense_part(
+    me, root, rp_ref, weight_ref, bias_ref, cot_ref, hid_ref, gt_ref, gsum_ref,
+    acc_ref, cs_ref, zs_ref, gl_ref, g1_ref, gz_ref, g2_ref,
 ):
-    me = Place(send_sem, recv_sem)
     core, mz = me.core, me.mz
-    met = me.enter([me.other] + [me.at_z(o) for o in range(1, NZ)])
-    root = lax.rsqrt(deg_ref[...].astype(F32))
-    met()
     plan = Plan()
     offsets = around(NZ)
     for i, o in enumerate(offsets):
@@ -443,8 +431,7 @@
 
     plan2.action(g2, after_z, (), 0.1)
     plan2.run()
-    plan.drain()
-    plan2.drain()
+    return [plan, plan2]
 
 
 def total_of(ref, n):
@@ -454,24 +441,8 @@
     return v
 
 
-COPIES3 = 76 + 3 + 7 + 7 + 1
-
-
-def scatter_body(
-    cp_ref, deg_ref, gsum_ref,
-    gf_ref, gw_ref, gb_ref,
-    acc_ref, sum_ref, g3_ref, g3x_ref, g4_ref, yx_ref, send_sem, recv_sem,
-):
-    me = Place(send_sem, recv_sem)
+def scatter_part(me, root, cp_ref, gsum_ref, gf_ref, gw_ref, gb_ref, acc_ref, sum_ref, g3_ref, g3x_ref, g4_ref, yx_ref):
     core, mz, mx, my = me.core, me.mz, me.mx, me.my
-    met = me.enter(
-        [me.other]
-        + [me.at_z(o) for o in range(1, NZ)]
-        + [me.at_xy(o, 0) for o in range(1, NX)]
-        + [me.at_xy(0, o) for o in range(1, NY)]
-    )
-    root = lax.rsqrt(deg_ref[...].astype(F32))
-    met()
     plan = Plan()
     slot_rows = [0]
 
@@ -573,93 +544,101 @@
     for h in range(2):
         v = yx_ref[h * T : (h + 1) * T, :] * root[h : h + 1, :]
         gf_ref[h * T : (h + 1) * T, :] = v.T.astype(BF16)
-    plan.drain()
-
-
-VMEM = pl.BlockSpec(memory_space=pltpu.VMEM)
-SMEM = pl.BlockSpec(memory_space=pltpu.SMEM)
+    return [plan]
+
+
+COPIES = 76 + 40 + 94
 ROW_NODES = PIECE * NZ * 2
 COL_NODES = PIECE * NX * NY
 
 
-def call(body, outs, ins, scratch, name, **params):
-    return pl.pallas_call(
+def body(
+    feat_ref, deg_ref, weight_ref, bias_ref, cot_ref, rows_ref, cols_ref, count_ref, codes_ref,
+    hid_ref, gf_ref, gw_ref, gb_ref,
+    xg_ref, masks_ref, tab_ref, at_ref, b_ref, pre_ref, rp_ref, racc_ref, cs_ref, zs_ref, gt_ref, cp_ref, cacc_ref,
+    sum_ref, gsum_ref, gl_ref, g1_ref, gz_ref, g2_ref, g3_ref, g3x_ref, g4_ref, yx_ref,
+    tab_s, tab_sem, send_sem, recv_sem,
+):
+    me = Place(send_sem, recv_sem)
+    met = me.enter([
+        me.at_xy(1, 0), me.at_xy(-1, 0), me.at_xy(0, 1), me.at_xy(0, -1), me.at_z(1), me.at_z(-1), me.other,
+    ])
+    root = lax.rsqrt(deg_ref[...].astype(F32))
+    tab_ref[...] = jnp.zeros_like(tab_ref)
+    plans = gather_part(
+        me, root, met, feat_ref, rows_ref, cols_ref, count_ref, codes_ref, xg_ref, masks_ref, tab_ref, at_ref, b_ref
+    )
+    moved = pltpu.make_async_copy(tab_ref, tab_s, tab_sem)
+    moved.start()
+    moved.wait()
+    product_part(True, ROW_NODES // T, tab_s, masks_ref, xg_ref, rp_ref, pre_ref)
+    plans += dense_part(
+        me, root, rp_ref, weight_ref, bias_ref, cot_ref, hid_ref, gt_ref, gsum_ref,
+        racc_ref, cs_ref, zs_ref, gl_ref, g1_ref, gz_ref, g2_ref,
+    )
+    product_part(False, COL_NODES // T, tab_s, masks_ref, gt_ref, cp_ref, pre_ref)
+    plans += scatter_part(
+        me, root, cp_ref, gsum_ref, gf_ref, gw_ref, gb_ref, cacc_ref, sum_ref, g3_ref, g3x_ref, g4_ref, yx_ref
+    )
+    for plan in plans:
+        plan.drain()
+
+
+def local(features, degree, weight, bias, cotangent, tile_rows, tile_cols, tile_count, tile_codes):
+    vmem = pl.BlockSpec(memory_space=pltpu.VMEM)
+    smem = pl.BlockSpec(memory_space=pltpu.SMEM)
+    hidden, grad_features, grad_weight, grad_bias = pl.pallas_call(
         body,
-        out_shape=tuple(jax.ShapeDtypeStruct(*o) for o in outs),
-        in_specs=ins,
-        out_specs=(VMEM,) * len(outs),
-        scratch_shapes=scratch,
-        compiler_params=pltpu.CompilerParams(**params),
-        name=name,
-    )
-
-
-def sems(n):
-    return [pltpu.SemaphoreType.DMA((n,)), pltpu.SemaphoreType.DMA((n,))]
-
-
-def local(features, degree, weight, bias, cotangent, tile_rows, tile_cols, tile_count, tile_codes):
-    degree = degree.reshape(2, T)
-    gather = call(
-        gather_body,
-        [((COL_NODES, T), BF16), ((SLOTS * T, T), BF16), ((16, T), I32)],
-        [VMEM] * 4 + [SMEM, VMEM],
-        [pltpu.VMEM((T, SLOTS), F32), pltpu.VMEM((SLOTS, T), F32)] + sems(COPIES1),
-        "gather", collective_id=0, has_side_effects=True,
-    )
-    gathered, masks, table = gather(
-        features, degree, tile_rows.reshape(1, SLOTS), tile_cols.reshape(1, SLOTS),
-        tile_count.reshape(1, 1), tile_codes.reshape(SLOTS, 2 * T),
-    )
-    forward = call(
-        functools.partial(product_body, True, ROW_NODES // T),
-        [((ROW_NODES, T), BF16)],
-        [SMEM, VMEM, VMEM],
-        [pltpu.VMEM((SLOTS * T, T), F32)],
-        "forward",
-    )
-    (row_terms,) = forward(table, masks, gathered)
-    dense = call(
-        dense_body,
-        [((PIECE, T), BF16), ((ROW_NODES, T), BF16), ((16, T), F32)],
-        [VMEM] * 5,
-        [
+        out_shape=(
+            jax.ShapeDtypeStruct((PIECE, T), BF16),
+            jax.ShapeDtypeStruct((PIECE, T), BF16),
+            jax.ShapeDtypeStruct((T, T), F32),
+            jax.ShapeDtypeStruct((1, T), F32),
+        ),
+        in_specs=[vmem] * 7 + [smem, vmem],
+        out_specs=(vmem,) * 4,
+        scratch_shapes=[
+            pltpu.VMEM((COL_NODES, T), BF16),
+            pltpu.VMEM((SLOTS * T, T), BF16),
+            pltpu.VMEM((16, T), I32),
+            pltpu.VMEM((T, SLOTS), F32),
+            pltpu.VMEM((SLOTS, T), F32),
+            pltpu.VMEM((SLOTS * T, T), F32),
+            pltpu.VMEM((ROW_NODES, T), BF16),
             pltpu.VMEM((ROW_NODES, T), BF16),
             pltpu.VMEM((PIECE * NZ, T), BF16),
             pltpu.VMEM((PIECE * (NZ - 1), T), BF16),
+            pltpu.VMEM((ROW_NODES, T), BF16),
+            pltpu.VMEM((COL_NODES, T), BF16),
+            pltpu.VMEM((COL_NODES, T), BF16),
+            pltpu.VMEM((COL_NODES - PIECE, T), BF16),
+            pltpu.VMEM((16, T), F32),
             pltpu.VMEM((144, T), F32),
             pltpu.VMEM((72, T), F32),
             pltpu.VMEM((16 * NZ, T), F32),
             pltpu.VMEM((16 * NZ, T), F32),
-        ]
-        + sems(COPIES2),
-        "dense", collective_id=1, has_side_effects=True,
-    )
-    hidden, grads_t, gsum = dense(row_terms, degree, weight, bias.reshape(1, T), cotangent)
-    backward = call(
-        functools.partial(product_body, False, COL_NODES // T),
-        [((COL_NODES, T), BF16)],
-        [SMEM, VMEM, VMEM],
-        [pltpu.VMEM((SLOTS * T, T), F32)],
-        "backward",
-    )
-    (col_terms,) = backward(table, masks, grads_t)
-    scatter = call(
-        scatter_body,
-        [((PIECE, T), BF16), ((T, T), F32), ((1, T), F32)],
-        [VMEM] * 3,
-        [
-            pltpu.VMEM((COL_NODES, T), BF16),
-            pltpu.VMEM((COL_NODES - PIECE, T), BF16),
             pltpu.VMEM((16 * NY, T), F32),
             pltpu.VMEM((16 * NX, T), F32),
             pltpu.VMEM((T, T), F32),
             pltpu.VMEM((PIECE, T), F32),
-        ]
-        + sems(COPIES3),
-        "scatter", collective_id=2, has_side_effects=True,
+            pltpu.SMEM((16, T), I32),
+            pltpu.SemaphoreType.DMA,
+            pltpu.SemaphoreType.DMA((COPIES,)),
+            pltpu.SemaphoreType.DMA((COPIES,)),
+        ],
+        compiler_params=pltpu.CompilerParams(collective_id=0, has_side_effects=True),
+        name="layer",
+    )(
+        features,
+        degree.reshape(2, T),
+        weight,
+        bias.reshape(1, T),
+        cotangent,
+        tile_rows.reshape(1, SLOTS),
+        tile_cols.reshape(1, SLOTS),
+        tile_count.reshape(1, 1),
+        tile_codes.reshape(SLOTS, 2 * T),
     )
-    grad_features, grad_weight, grad_bias = scatter(col_terms, degree, gsum)
     return hidden, grad_features, grad_weight, grad_bias.reshape(T)
 
 

time: 137 us -> 116 us (0.85)
  the two profiles are of different devices: /device:TPU:1 before, /device:TPU:16 now
where the time goes in v2:
time: 116 us; the launch traced here: 115 us
  Pallas kernels  110 us (95%)
  local copies, waits for them, and re-layouts  3.55 us (3%)
  between operations  1.3 us (1%)
    pallas_call x1, Pallas kernels, local(): pl.pallas_call(body, out_shape=(jax.ShapeDtypeStruct((PIECE, T), BF16), j...  110 us
    unnamed x10, local copies, waits for them, and re-layouts  3.55 us

profile of v2, /device:TPU:16, one launch (start us, length us, event | category | flops | bytes accessed | tf_op | source)
XLA Modules:
  0.0 115.3 jit_solution(8024725918359332012)
XLA Ops:
  1.3 110.5 %layer.1 = (bf16[256,128]{1,0:T(8,128)(2,1)}, bf16[256,128]{1,0:T(8,128)(2,1)}, f32[128,128]{1,0:T(8,128)}, f32[1,128]{1,0:T(1,128)}) custom-call(bf16[256,128]{1,0:T(8,128)(2,1)} %feat_ref.1, s32[2,128]{1,0:T(2,128)} %bitcast.9, bf16[128,128]{1,0:T(8,128)(2,1)} %weight_ref.1, f32[1,128]{1,0:T(1,128)} %bitcast.10, bf16[256,128]{1,0:T(8,128)(2,1)} %cot_ref.1, ...), custom_call_target="tpu_custom_call" | custom-call | tf_op jit(solution)/shard_map/layer/pallas_call | solution.py:590
  111.7 0.0 copy-start.1
  111.8 1.5 %copy.18 = bf16[256,128]{1,0:T(8,128)(2,1)} copy(bf16[256,128]{1,0:T(8,128)(2,1)} %get-tuple-element.16) | data formatting | bytes 131072
  113.3 0.0 copy-done.1
  113.3 0.0 copy-start
  113.3 0.6 copy.19
  113.9 0.2 copy-done
  114.1 0.0 copy-start.2
  114.1 0.6 copy.20
  114.8 0.0 copy-done.2
  114.8 0.5 copy.21
Async XLA Ops:
  111.7 1.5 %copy-start.1 = (bf16[256,128]{1,0:T(8,128)(2,1)S(1)}, bf16[256,128]{1,0:T(8,128)(2,1)}, u32[]{:S(2)}) copy-start(bf16[256,128]{1,0:T(8,128)(2,1)} %get-tuple-element.17) | copy-start | bytes 196612
  113.3 0.9 copy-start
  114.1 0.7 copy-start.2

commit v3 on v2

--- a/solution.py
+++ b/solution.py
@@ -23,7 +23,8 @@
 
 WIRE = 46e3
 CORE_WIRE = 250e3
-HOP = 1.7
+HOP = 2.5
+HOP_MORE = 0.5
 CORE_HOP = 0.95
 
 
@@ -76,8 +77,10 @@
                 copy = make()
                 self.copies[key][3] = copy
                 copy.start()
-                wire, hop = (CORE_WIRE, CORE_HOP) if link[0] == "c" else (WIRE, HOP)
-                free[link] = max(free.get(link, 0.0), now) + nbytes / wire
+                hops = link[2] if len(link) > 2 else 1
+                wire, hop = (CORE_WIRE, CORE_HOP) if link[0] == "c" else (WIRE, HOP + HOP_MORE * (hops - 1))
+                link = link[:2]
+                free[link] = max(free.get(link, 0.0), now) + nbytes * hops / wire
                 arrival[key] = free[link] + hop
         for fn, cost in fill:
             fn()
@@ -170,6 +173,14 @@
         dst[rows_of(piece, f, n), :] = v.astype(BF16)
 
 
+CHAIN4 = ((0, 1), (1, 1))
+DIRECT4 = ((0, 1), (0, 2))
+CHAIN8 = ((0, 1), (1, 1), (2, 1), (3, 1))
+TWO8 = ((0, 2), (0, 1), (2, 2), (2, 1))
+STEPS = {("A", "x"): DIRECT4, ("A", "y"): TWO8, ("B", "y"): TWO8, ("B", "x"): CHAIN4}
+STEPS_Z = TWO8
+
+
 def around(n):
     out = [n // 2]
     for k in range(n // 2 - 1, 0, -1):
@@ -184,41 +195,34 @@
     met()
     plan = Plan()
 
-    def leg(which, axis, o, d, k):
+    def leg(which, axis, o, d, b, h):
         n = NX if axis == "x" else NY
-        first, size = part_rows(which, d, k == n // 2)
-        back = -d * (k - 1)
-        piece = me.xy_piece(back, o) if axis == "x" else me.xy_piece(o, back)
+        first, size = part_rows(which, d, b + h == n // 2)
+        piece = me.xy_piece(-d * b, o) if axis == "x" else me.xy_piece(o, -d * b)
         where = lambda: xg_ref.at[rows_of(piece, first, size), :]
-        dev = me.at_xy(d, 0) if axis == "x" else me.at_xy(0, d)
-        key = (which, axis, o, d, k)
-        plan.message(key, (axis, d), size * 256, me.copier(where, where, dev))
+        dev = me.at_xy(d * h, 0) if axis == "x" else me.at_xy(0, d * h)
+        key = (which, axis, o, d, b + h)
+        plan.message(key, (axis, d, h), size * 256, me.copier(where, where, dev))
         return key
 
+    for which, one in (("A", "x"), ("B", "y")):
+        for b, h in STEPS[which, one]:
+            for d in (1, -1):
+                need = [(which, one, 0, d, b)] if b else []
+                plan.action(need, None, [leg(which, one, 0, d, b, h)])
     for which, one, two in (("A", "x", "y"), ("B", "y", "x")):
         n1 = NX if one == "x" else NY
-        n2 = NX if two == "x" else NY
-        legs = {}
-        for d in (1, -1):
-            for k in range(1, n1 // 2 + 1):
-                legs[d, k] = leg(which, one, 0, d, k)
-        for d in (1, -1):
-            plan.action([], None, [legs[d, 1]])
-            for k in range(2, n1 // 2 + 1):
-                plan.action([legs[d, k - 1]], None, [legs[d, k]])
-        for o in range(-(n1 // 2) + 1, n1 // 2 + 1):
+        for o in around(n1)[::-1]:
             if o == 0:
-                need = []
+                have = []
             elif o == n1 // 2:
-                need = [legs[1, o], legs[-1, o]]
+                have = [(which, one, 0, 1, o), (which, one, 0, -1, o)]
             else:
-                need = [legs[-1 if o > 0 else 1, abs(o)]]
-            for d in (1, -1):
-                before = need
-                for k in range(1, n2 // 2 + 1):
-                    key = leg(which, two, o, d, k)
-                    plan.action(before, None, [key])
-                    before = [key]
+                have = [(which, one, 0, -1 if o > 0 else 1, abs(o))]
+            for b, h in STEPS[which, two]:
+                for d in (1, -1):
+                    need = [(which, two, o, d, b)] if b else have
+                    plan.action(need, None, [leg(which, two, o, d, b, h)])
 
     def tables():
         lane = lax.broadcasted_iota(I32, (T, T), 1)
@@ -320,42 +324,38 @@
     legs = {}
     base = 0
     for d in (1, -1):
-        for k in range(NZ // 2, 0, -1):
-            first, size = (0, PIECE) if k < NZ // 2 else half(0, PIECE, d)
-            piece = me.z_piece(d * k, core)
-            legs[d, k] = (base, first, size, piece)
+        for b, h in STEPS_Z:
+            first, size = half(0, PIECE, d) if b + h == NZ // 2 else (0, PIECE)
+            piece = me.z_piece(d * (b + h), core)
+            legs[d, b, h] = (base, first, size, piece)
             plan.message(
-                ("z", d, k), ("z", d), size * 256,
+                ("z", d, b, h), ("z", d, h), size * 256,
                 me.copier(
                     functools.partial(lambda p, f, s: acc_ref.at[rows_of(p, f, s), :], piece, first, size),
                     functools.partial(lambda b, s: zs_ref.at[pl.ds(b, s), :], base, size),
-                    me.at_z(d),
+                    me.at_z(d * h),
                 ),
             )
             base += size
 
-    def z_add(d, k):
-        o = NZ // 2 if k == NZ // 2 else d * k
-        _, first, size, piece = legs[d, k]
-        given = [(cs_ref, offsets.index(o) * PIECE + first, first, size)]
-        if k < NZ // 2:
-            b, f, n, _ = legs[d, k + 1]
-            given.append((zs_ref, b, f, n))
+    def z_add(d, b, h, before):
+        o = NZ // 2 if b + h == NZ // 2 else d * (b + h)
+        _, first, size, piece = legs[d, b, h]
+        given = [(cs_ref, offsets.index(o) * PIECE, 0, PIECE)] + [(zs_ref,) + legs[k][:3] for k in before]
         combine(acc_ref, rp_ref, piece, first, size, given)
 
-    for k in range(NZ // 2, 0, -1):
+    for b, h in sorted(STEPS_Z, key=lambda s: (-s[0], -s[1])):
         for d in (1, -1):
-            deps = [("c", NZ // 2 if k == NZ // 2 else d * k)]
-            if k < NZ // 2:
-                deps.append(("z", d, k + 1))
-            plan.action(deps, functools.partial(z_add, d, k), [("z", d, k)], 0.08)
+            before = [(d, b2, h2) for b2, h2 in STEPS_Z if b2 == b + h]
+            deps = [("c", NZ // 2 if b + h == NZ // 2 else d * (b + h))] + [("z",) + k for k in before]
+            plan.action(deps, functools.partial(z_add, d, b, h, before), [("z", d, b, h)], 0.1)
     plan.run()
 
     i0 = offsets.index(0)
     agg_sum = rp_ref[rows_of(me.col, 0, PIECE), :].astype(F32) + cs_ref[i0 * PIECE : (i0 + 1) * PIECE, :].astype(F32)
-    for d in (1, -1):
-        b = legs[d, 1][0]
-        agg_sum = agg_sum + zs_ref[b : b + PIECE, :].astype(F32)
+    for (d, b, h), (base, _, size, _) in legs.items():
+        if b == 0:
+            agg_sum = agg_sum + zs_ref[base : base + PIECE, :].astype(F32)
     spread = jnp.concatenate([jnp.broadcast_to(root[h : h + 1, :], (T, T)).T for h in range(2)], axis=0)
     aggregate = (spread * agg_sum).astype(BF16)
     weight = weight_ref[...]
@@ -369,19 +369,17 @@
         gt_ref[rows_of(me.col, h * T, T), :] = (grad_agg_t[:, h * T : (h + 1) * T] * root[h : h + 1, :]).astype(BF16)
 
     plan2 = Plan()
-    for d in (1, -1):
-        for k in range(1, NZ // 2 + 1):
-            first, size = (0, PIECE) if k < NZ // 2 else half(0, PIECE, d)
-            piece = me.z_piece(-d * (k - 1), core)
+    for b, h in STEPS_Z:
+        for d in (1, -1):
+            first, size = half(0, PIECE, d) if b + h == NZ // 2 else (0, PIECE)
+            piece = me.z_piece(-d * b, core)
             where = functools.partial(lambda p, f, s: gt_ref.at[rows_of(p, f, s), :], piece, first, size)
-            plan2.message(("Z", d, k), ("z", d), size * 256, me.copier(where, where, me.at_z(d)))
+            plan2.message(("Z", d, b + h), ("z", d, h), size * 256, me.copier(where, where, me.at_z(d * h)))
+            plan2.action([("Z", d, b)] if b else [], None, [("Z", d, b + h)])
     for o in offsets:
         where = functools.partial(lambda p: gt_ref.at[rows_of(p, 0, PIECE), :], me.z_piece(o, core))
         plan2.message(("C", o), ("c", 1), 65536, me.copier(where, where, me.other))
-    plan2.action([], None, [("Z", 1, 1), ("Z", -1, 1), ("C", 0)])
-    for d in (1, -1):
-        for k in range(2, NZ // 2 + 1):
-            plan2.action([("Z", d, k - 1)], None, [("Z", d, k)])
+    plan2.action([], None, [("C", 0)])
     for k in range(1, NZ // 2 + 1):
         if k == NZ // 2:
             plan2.action([("Z", 1, k), ("Z", -1, k)], None, [("C", k)])
@@ -446,16 +444,16 @@
     plan = Plan()
     slot_rows = [0]
 
-    def leg(which, axis, o, d, k, src):
+    def leg(which, axis, o, d, b, h, src):
         n = NX if axis == "x" else NY
-        first, size = part_rows(which, d, k == n // 2)
-        piece = me.xy_piece(d * k, o) if axis == "x" else me.xy_piece(o, d * k)
+        first, size = part_rows(which, d, b + h == n // 2)
+        piece = me.xy_piece(d * (b + h), o) if axis == "x" else me.xy_piece(o, d * (b + h))
         base = slot_rows[0]
         slot_rows[0] += size
-        dev = me.at_xy(d, 0) if axis == "x" else me.at_xy(0, d)
-        key = ("s", which, axis, o, d, k)
+        dev = me.at_xy(d * h, 0) if axis == "x" else me.at_xy(0, d * h)
+        key = ("s", which, axis, o, d, b, h)
         plan.message(
-            key, (axis, d), size * 256,
+            key, (axis, d, h), size * 256,
             me.copier(
                 lambda: src.at[rows_of(piece, first, size), :], lambda: sum_ref.at[pl.ds(base, size), :], dev
             ),
@@ -470,30 +468,36 @@
 
     finals = {}
     late = []
+    first_sends = []
     for which, one, two in (("A", "y", "x"), ("B", "x", "y")):
-        n1 = NX if one == "x" else NY
         n2 = NX if two == "x" else NY
         done = {}
+        steps = sorted(STEPS[which, one], key=lambda s: (-s[0], -s[1]))
         for o in around(n2):
-            ends = []
+            done[o] = []
             for d in (1, -1):
-                prev = None
-                for k in range(n1 // 2, 0, -1):
-                    now = leg(which, one, o, d, k, cp_ref if prev is None else acc_ref)
-                    if prev is None:
-                        plan.action([], None, [now["key"]])
+                made = {}
+                for b, h in steps:
+                    prev = [made[k] for k in made if k[0] == b + h]
+                    now = made[b, h] = leg(which, one, o, d, b, h, acc_ref if prev else cp_ref)
+                    if prev:
+                        late.append(([e["key"] for e in prev], adder(now, *prev), [now["key"]], 0.06))
                     else:
-                        late.append(([prev["key"]], adder(now, prev), [now["key"]], 0.05))
-                    prev = now
-                ends.append(prev)
-            done[o] = ends
-        legs = {}
+                        first_sends.append((b, now["key"]))
+                    if b == 0:
+                        done[o].append(now)
+        finals[which] = list(done[0])
         for d in (1, -1):
-            for k in range(n2 // 2, 0, -1):
-                now = legs[d, k] = leg(which, two, 0, d, k, acc_ref)
-                more = done[n2 // 2 if k == n2 // 2 else d * k] + ([legs[d, k + 1]] if k < n2 // 2 else [])
+            made = {}
+            for b, h in sorted(STEPS[which, two], key=lambda s: (-s[0], -s[1])):
+                prev = [made[k] for k in made if k[0] == b + h]
+                now = made[b, h] = leg(which, two, 0, d, b, h, acc_ref)
+                more = done[n2 // 2 if b + h == n2 // 2 else d * (b + h)] + prev
                 late.append(([e["key"] for e in more], adder(now, *more), [now["key"]], 0.08))
-        finals[which] = done[0] + [legs[1, 1], legs[-1, 1]]
+                if b == 0:
+                    finals[which].append(now)
+    for _, key in sorted(first_sends, key=lambda e: -e[0]):
+        plan.action([], None, [key])
     for deps, fn, sends, cost in late:
         plan.action(deps, fn, sends, cost)
 
@@ -535,12 +539,10 @@
     plan.action([("G5", 0)], give_weight, (), 0.05)
     plan.run()
 
-    for which in ("A", "B"):
-        first, size = PARTS[which]
-        v = cp_ref[rows_of(me.row, first, size), :].astype(F32)
-        for e in finals[which]:
-            v = v + sum_ref[pl.ds(e["base"], e["size"]), :].astype(F32)
-        yx_ref[first : first + size, :] = v
+    yx_ref[...] = cp_ref[rows_of(me.row, 0, PIECE), :].astype(F32)
+    for e in finals["A"] + finals["B"]:
+        at = slice(e["first"], e["first"] + e["size"])
+        yx_ref[at, :] = yx_ref[at, :] + sum_ref[pl.ds(e["base"], e["size"]), :].astype(F32)
     for h in range(2):
         v = yx_ref[h * T : (h + 1) * T, :] * root[h : h + 1, :]
         gf_ref[h * T : (h + 1) * T, :] = v.T.astype(BF16)
@@ -560,9 +562,12 @@
     tab_s, tab_sem, send_sem, recv_sem,
 ):
     me = Place(send_sem, recv_sem)
-    met = me.enter([
-        me.at_xy(1, 0), me.at_xy(-1, 0), me.at_xy(0, 1), me.at_xy(0, -1), me.at_z(1), me.at_z(-1), me.other,
-    ])
+    met = me.enter(
+        [me.at_xy(o, 0) for o in (1, 2, 3)]
+        + [me.at_xy(0, o) for o in (1, 2, -2, -1)]
+        + [me.at_z(o) for o in (1, 2, -2, -1)]
+        + [me.other]
+    )
     root = lax.rsqrt(deg_ref[...].astype(F32))
     tab_ref[...] = jnp.zeros_like(tab_ref)
     plans = gather_part(

time: 116 us -> 104 us (0.90)
  the two profiles are of different devices: /device:TPU:16 before, /device:TPU:1 now
where the time goes in v3:
time: 104 us
  Pallas kernels  99 us (95%)
  local copies, waits for them, and re-layouts  3.55 us (3%)
  between operations  1.3 us (1%)
    pallas_call x1, Pallas kernels, local(): pl.pallas_call(body, out_shape=(jax.ShapeDtypeStruct((PIECE, T), BF16), j...  99 us
    unnamed x10, local copies, waits for them, and re-layouts  3.55 us

profile of v3, /device:TPU:1, one launch (start us, length us, event | category | flops | bytes accessed | tf_op | source)
XLA Modules:
  0.0 103.9 jit_solution(3574872660859401953)
XLA Ops:
  1.3 99.0 %layer.1 = (bf16[256,128]{1,0:T(8,128)(2,1)}, bf16[256,128]{1,0:T(8,128)(2,1)}, f32[128,128]{1,0:T(8,128)}, f32[1,128]{1,0:T(1,128)}) custom-call(bf16[256,128]{1,0:T(8,128)(2,1)} %feat_ref.1, s32[2,128]{1,0:T(2,128)} %bitcast.9, bf16[128,128]{1,0:T(8,128)(2,1)} %weight_ref.1, f32[1,128]{1,0:T(1,128)} %bitcast.10, bf16[256,128]{1,0:T(8,128)(2,1)} %cot_ref.1, ...), custom_call_target="tpu_custom_call" | custom-call | tf_op jit(solution)/shard_map/layer/pallas_call | solution.py:595
  100.3 0.0 copy-start.1
  100.3 1.5 %copy.18 = bf16[256,128]{1,0:T(8,128)(2,1)} copy(bf16[256,128]{1,0:T(8,128)(2,1)} %get-tuple-element.16) | data formatting | bytes 131072
  101.8 0.0 copy-done.1
  101.8 0.0 copy-start
  101.8 0.6 copy.19
  102.5 0.2 copy-done
  102.7 0.0 copy-start.2
  102.7 0.6 copy.20
  103.3 0.0 copy-done.2
  103.4 0.5 copy.21
Async XLA Ops:
  100.3 1.5 %copy-start.1 = (bf16[256,128]{1,0:T(8,128)(2,1)S(1)}, bf16[256,128]{1,0:T(8,128)(2,1)}, u32[]{:S(2)}) copy-start(bf16[256,128]{1,0:T(8,128)(2,1)} %get-tuple-element.17) | copy-start | bytes 196612
  101.8 0.9 copy-start
  102.7 0.7 copy-start.2

commit v4 on v3

--- a/solution.py
+++ b/solution.py
@@ -19,7 +19,7 @@
 SLOTS = 128
 PRIME = 4093
 ROUND = 12582912.0
-CUT = 96
+CUT = 128
 
 WIRE = 46e3
 CORE_WIRE = 250e3
@@ -281,7 +281,7 @@
     return pl.ds(t * T, T)
 
 
-def product_part(forward, tiles, tab_ref, masks_ref, src_ref, out_ref, pre_ref):
+def product_part(forward, tab_ref, masks_ref, src_ref, out_ref, pre_ref):
     base = 0 if forward else 5
 
     def step(g, acc):
@@ -295,67 +295,81 @@
         return acc
 
     lax.fori_loop(0, SLOTS // UNROLL, step, jnp.zeros((T, T), F32))
-    for t in range(tiles):
+
+    def form(t):
         v = pre_ref[tile_at(tab_ref[base + 3, t]), :]
-        out_ref[t * T : (t + 1) * T, :] = (v * tab_ref[base + 4, t].astype(F32)).astype(BF16)
+        out_ref[tile_rows(t), :] = (v * tab_ref[base + 4, t].astype(F32)).astype(BF16)
+
+    return form
 
 
 W1 = T // 2
-WZ = W1 // NZ
+WY = W1 // NY
 
 
 def dense_part(
-    me, root, rp_ref, weight_ref, bias_ref, cot_ref, hid_ref, gt_ref, gsum_ref,
-    acc_ref, cs_ref, zs_ref, gl_ref, g1_ref, gz_ref, g2_ref,
+    me, root, form, rp_ref, weight_ref, bias_ref, cot_ref, hid_ref, gt_ref, gsum_ref,
+    acc_ref, cs_ref, zs_ref, gl_ref, g1_ref, gz_ref, g2_ref, g3x_ref,
 ):
-    core, mz = me.core, me.mz
+    core, mx, my = me.core, me.mx, me.my
     plan = Plan()
     offsets = around(NZ)
-    for i, o in enumerate(offsets):
-        plan.message(
-            ("c", o), ("c", 1), 65536,
-            me.copier(
-                functools.partial(lambda p: rp_ref.at[rows_of(p, 0, PIECE), :], me.z_piece(o, 1 - core)),
-                functools.partial(lambda i: cs_ref.at[pl.ds(i * PIECE, PIECE), :], i),
-                me.other,
-            ),
-        )
-        plan.action([], None, [("c", o)], 0.05)
+    chunks = [(c, c * T, T) for c in range(PIECE // T)]
+    for c, first, size in chunks:
+        for i, o in enumerate(offsets):
+            theirs = me.z_piece(o, 1 - core)
+            plan.message(
+                ("c", o, c), ("c", 1), size * 256,
+                me.copier(
+                    functools.partial(lambda p, f, s: rp_ref.at[rows_of(p, f, s), :], theirs, first, size),
+                    functools.partial(lambda f, s: cs_ref.at[pl.ds(f, s), :], i * PIECE + first, size),
+                    me.other,
+                ),
+            )
+            plan.action([], functools.partial(form, theirs * 2 + c), [("c", o, c)], 0.03)
+    for c, _, _ in chunks:
+        for o in offsets:
+            plan.action([], functools.partial(form, me.z_piece(o, core) * 2 + c), (), 0.03)
     legs = {}
     base = 0
     for d in (1, -1):
         for b, h in STEPS_Z:
-            first, size = half(0, PIECE, d) if b + h == NZ // 2 else (0, PIECE)
-            piece = me.z_piece(d * (b + h), core)
-            legs[d, b, h] = (base, first, size, piece)
-            plan.message(
-                ("z", d, b, h), ("z", d, h), size * 256,
-                me.copier(
-                    functools.partial(lambda p, f, s: acc_ref.at[rows_of(p, f, s), :], piece, first, size),
-                    functools.partial(lambda b, s: zs_ref.at[pl.ds(b, s), :], base, size),
-                    me.at_z(d * h),
-                ),
-            )
-            base += size
-
-    def z_add(d, b, h, before):
+            for c, first, size in chunks:
+                if b + h == NZ // 2:
+                    first, size = half(first, size, d)
+                piece = me.z_piece(d * (b + h), core)
+                legs[d, b, h, c] = (base, first, size, piece)
+                plan.message(
+                    ("z", d, b, h, c), ("z", d, h), size * 256,
+                    me.copier(
+                        functools.partial(lambda p, f, s: acc_ref.at[rows_of(p, f, s), :], piece, first, size),
+                        functools.partial(lambda b, s: zs_ref.at[pl.ds(b, s), :], base, size),
+                        me.at_z(d * h),
+                    ),
+                )
+                base += size
+
+    def z_add(d, b, h, c, before):
         o = NZ // 2 if b + h == NZ // 2 else d * (b + h)
-        _, first, size, piece = legs[d, b, h]
+        _, first, size, piece = legs[d, b, h, c]
         given = [(cs_ref, offsets.index(o) * PIECE, 0, PIECE)] + [(zs_ref,) + legs[k][:3] for k in before]
         combine(acc_ref, rp_ref, piece, first, size, given)
 
-    for b, h in sorted(STEPS_Z, key=lambda s: (-s[0], -s[1])):
-        for d in (1, -1):
-            before = [(d, b2, h2) for b2, h2 in STEPS_Z if b2 == b + h]
-            deps = [("c", NZ // 2 if b + h == NZ // 2 else d * (b + h))] + [("z",) + k for k in before]
-            plan.action(deps, functools.partial(z_add, d, b, h, before), [("z", d, b, h)], 0.1)
+    for c, _, _ in chunks:
+        for b, h in sorted(STEPS_Z, key=lambda s: (-s[0], -s[1])):
+            for d in (1, -1):
+                before = [(d, b2, h2, c) for b2, h2 in STEPS_Z if b2 == b + h]
+                deps = [("c", NZ // 2 if b + h == NZ // 2 else d * (b + h), c)] + [("z",) + k for k in before]
+                plan.action(deps, functools.partial(z_add, d, b, h, c, before), [("z", d, b, h, c)], 0.06)
     plan.run()
 
     i0 = offsets.index(0)
     agg_sum = rp_ref[rows_of(me.col, 0, PIECE), :].astype(F32) + cs_ref[i0 * PIECE : (i0 + 1) * PIECE, :].astype(F32)
-    for (d, b, h), (base, _, size, _) in legs.items():
-        if b == 0:
-            agg_sum = agg_sum + zs_ref[base : base + PIECE, :].astype(F32)
+    for d in (1, -1):
+        for b, h in STEPS_Z:
+            if b == 0:
+                got = [zs_ref[pl.ds(legs[d, b, h, c][0], size), :] for c, _, size in chunks]
+                agg_sum = agg_sum + jnp.concatenate([g.astype(F32) for g in got], axis=0)
     spread = jnp.concatenate([jnp.broadcast_to(root[h : h + 1, :], (T, T)).T for h in range(2)], axis=0)
     aggregate = (spread * agg_sum).astype(BF16)
     weight = weight_ref[...]
@@ -369,23 +383,25 @@
         gt_ref[rows_of(me.col, h * T, T), :] = (grad_agg_t[:, h * T : (h + 1) * T] * root[h : h + 1, :]).astype(BF16)
 
     plan2 = Plan()
-    for b, h in STEPS_Z:
-        for d in (1, -1):
-            first, size = half(0, PIECE, d) if b + h == NZ // 2 else (0, PIECE)
-            piece = me.z_piece(-d * b, core)
-            where = functools.partial(lambda p, f, s: gt_ref.at[rows_of(p, f, s), :], piece, first, size)
-            plan2.message(("Z", d, b + h), ("z", d, h), size * 256, me.copier(where, where, me.at_z(d * h)))
-            plan2.action([("Z", d, b)] if b else [], None, [("Z", d, b + h)])
-    for o in offsets:
-        where = functools.partial(lambda p: gt_ref.at[rows_of(p, 0, PIECE), :], me.z_piece(o, core))
-        plan2.message(("C", o), ("c", 1), 65536, me.copier(where, where, me.other))
-    plan2.action([], None, [("C", 0)])
-    for k in range(1, NZ // 2 + 1):
-        if k == NZ // 2:
-            plan2.action([("Z", 1, k), ("Z", -1, k)], None, [("C", k)])
-        else:
+    for c, first, size in chunks:
+        for b, h in STEPS_Z:
             for d in (1, -1):
-                plan2.action([("Z", d, k)], None, [("C", -d * k)])
+                f, n = half(first, size, d) if b + h == NZ // 2 else (first, size)
+                piece = me.z_piece(-d * b, core)
+                where = functools.partial(lambda p, f, s: gt_ref.at[rows_of(p, f, s), :], piece, f, n)
+                plan2.message(("Z", d, b + h, c), ("z", d, h), n * 256, me.copier(where, where, me.at_z(d * h)))
+                plan2.action([("Z", d, b, c)] if b else [], None, [("Z", d, b + h, c)])
+    for c, first, size in chunks:
+        for o in offsets:
+            where = functools.partial(lambda p, f, s: gt_ref.at[rows_of(p, f, s), :], me.z_piece(o, core), first, size)
+            plan2.message(("C", o, c), ("c", 1), size * 256, me.copier(where, where, me.other))
+        plan2.action([], None, [("C", 0, c)])
+        for k in range(1, NZ // 2 + 1):
+            if k == NZ // 2:
+                plan2.action([("Z", 1, k, c), ("Z", -1, k, c)], None, [("C", k, c)])
+            else:
+                for d in (1, -1):
+                    plan2.action([("Z", d, k, c)], None, [("C", -d * k, c)])
 
     scale = 1.0 / math.sqrt(PIECE * NX * NY * NZ * 2)
 
@@ -404,30 +420,40 @@
     )
     plan2.action([], grads, [("G", 1)], 0.5)
     g2 = []
-    for o in range(1, NZ):
+    for o in range(1, NY):
         g2.append(("G2", o))
         plan2.message(
-            ("G2", o), ("gz", o), 16 * 512,
+            ("G2", o), ("gy", o), 16 * 512,
             me.copier(
-                functools.partial(lambda o: gz_ref.at[slots_of(lax.rem(mz + o, NZ), 16), :], o),
-                lambda: g2_ref.at[slots_of(mz, 16), :],
-                me.at_z(o),
+                functools.partial(lambda o: gz_ref.at[slots_of(lax.rem(my + o, NY), 16), :], o),
+                lambda: g2_ref.at[slots_of(my, 16), :],
+                me.at_xy(0, o),
             ),
         )
 
     def after_chip():
         total = gl_ref[slots_of(core, 72), :] + g1_ref[...]
-        for z in range(NZ):
-            gz_ref[z * 16 : z * 16 + 8, :] = total[z * WZ : (z + 1) * WZ, :]
-            gz_ref[z * 16 + 8 : z * 16 + 16, :] = total[W1 : W1 + 8, :]
-        g2_ref[slots_of(mz, 16), :] = gz_ref[slots_of(mz, 16), :]
+        for y in range(NY):
+            gz_ref[y * 16 : y * 16 + 8, :] = total[y * WY : (y + 1) * WY, :]
+            gz_ref[y * 16 + 8 : y * 16 + 16, :] = total[W1 : W1 + 8, :]
+        g2_ref[slots_of(my, 16), :] = gz_ref[slots_of(my, 16), :]
 
     plan2.action([("G", 1)], after_chip, g2, 0.2)
-
-    def after_z():
-        gsum_ref[...] = total_of(g2_ref, NZ)
-
-    plan2.action(g2, after_z, (), 0.1)
+    own_x = lambda: g3x_ref.at[slots_of(mx, 16), :]
+    g3x = []
+    for o in range(1, NX):
+        g3x.append(("G3x", o))
+        plan2.message(("G3x", o), ("gx", o), 16 * 512, me.copier(own_x, own_x, me.at_xy(o, 0)))
+
+    def after_y():
+        g3x_ref[slots_of(mx, 16), :] = total_of(g2_ref, NY)
+
+    plan2.action(g2, after_y, g3x, 0.1)
+
+    def after_x():
+        gsum_ref[...] = total_of(g3x_ref, NX)
+
+    plan2.action(g3x, after_x, (), 0.05)
     plan2.run()
     return [plan, plan2]
 
@@ -439,8 +465,8 @@
     return v
 
 
-def scatter_part(me, root, cp_ref, gsum_ref, gf_ref, gw_ref, gb_ref, acc_ref, sum_ref, g3_ref, g3x_ref, g4_ref, yx_ref):
-    core, mz, mx, my = me.core, me.mz, me.mx, me.my
+def scatter_part(me, root, form, cp_ref, gsum_ref, gf_ref, gw_ref, gb_ref, acc_ref, sum_ref, g3_ref, g4_ref, yx_ref):
+    core, mz, my = me.core, me.mz, me.my
     plan = Plan()
     slot_rows = [0]
 
@@ -458,7 +484,8 @@
                 lambda: src.at[rows_of(piece, first, size), :], lambda: sum_ref.at[pl.ds(base, size), :], dev
             ),
         )
-        return dict(key=key, base=base, first=first, size=size, piece=piece)
+        at = (d * (b + h), o) if axis == "x" else (o, d * (b + h))
+        return dict(key=key, base=base, first=first, size=size, piece=piece, at=at)
 
     def given(*legs):
         return [(sum_ref, e["base"], e["first"], e["size"]) for e in legs]
@@ -483,7 +510,7 @@
                     if prev:
                         late.append(([e["key"] for e in prev], adder(now, *prev), [now["key"]], 0.06))
                     else:
-                        first_sends.append((b, now["key"]))
+                        first_sends.append((b, now))
                     if b == 0:
                         done[o].append(now)
         finals[which] = list(done[0])
@@ -496,8 +523,20 @@
                 late.append(([e["key"] for e in more], adder(now, *more), [now["key"]], 0.08))
                 if b == 0:
                     finals[which].append(now)
-    for _, key in sorted(first_sends, key=lambda e: -e[0]):
-        plan.action([], None, [key])
+    formed = []
+
+    def form_rows(leg):
+        x, y = leg["at"]
+        for h in range(2):
+            if leg["first"] < (h + 1) * T and leg["first"] + leg["size"] > h * T and (x % NX, y % NY, h) not in formed:
+                formed.append((x % NX, y % NY, h))
+                form(me.xy_piece(x % NX, y % NY) * 2 + h)
+
+    for _, leg_now in sorted(first_sends, key=lambda e: -e[0]):
+        plan.action([], functools.partial(form_rows, leg_now), [leg_now["key"]], 0.04)
+    for x in range(NX):
+        for y in range(NY):
+            plan.action([], functools.partial(form_rows, dict(at=(x, y), first=0, size=PIECE)), (), 0.04)
     for deps, fn, sends, cost in late:
         plan.action(deps, fn, sends, cost)
 
@@ -508,27 +547,21 @@
             plan.message((tag, o), (tag, o), size * 512, me.copier(where, where, dev(o)))
         return keys
 
-    g3x = ride("G3x", NX, lambda o: me.at_xy(o, 0), lambda: g3x_ref.at[slots_of(mx, 16), :], 16)
-
-    def start_x():
-        g3x_ref[slots_of(mx, 16), :] = gsum_ref[...]
-
-    plan.action([], start_x, g3x, 0.02)
-    g3y = ride("G3y", NY, lambda o: me.at_xy(0, o), lambda: g3_ref.at[slots_of(my, 16), :], 16)
-
-    def after_x():
-        g3_ref[slots_of(my, 16), :] = total_of(g3x_ref, NX)
-
-    plan.action(g3x, after_x, g3y, 0.05)
-    own_w = lambda: pl.ds(pl.multiple_of(core * W1 + mz * WZ, 8), WZ)
-    g4 = ride("G4", NZ, me.at_z, lambda: g4_ref.at[own_w(), :], WZ)
-
-    def after_y():
-        v = total_of(g3_ref, NY)
+    g3z = ride("G3z", NZ, me.at_z, lambda: g3_ref.at[slots_of(mz, 16), :], 16)
+
+    def start_z():
+        g3_ref[slots_of(mz, 16), :] = gsum_ref[...]
+
+    plan.action([], start_z, g3z, 0.02)
+    own_w = lambda: pl.ds(pl.multiple_of(core * W1 + my * WY, 8), WY)
+    g4 = ride("G4", NY, lambda o: me.at_xy(0, o), lambda: g4_ref.at[own_w(), :], WY)
+
+    def after_z():
+        v = total_of(g3_ref, NZ)
         gb_ref[...] = v[8:9, :]
         g4_ref[own_w(), :] = v[0:8, :]
 
-    plan.action(g3y, after_y, g4, 0.05)
+    plan.action(g3z, after_z, g4, 0.05)
     half_w = lambda: g4_ref.at[slots_of(core, W1), :]
     plan.message(("G5", 0), ("c", 1), W1 * 512, me.copier(half_w, half_w, me.other))
     plan.action(g4, None, [("G5", 0)])
@@ -549,7 +582,7 @@
     return [plan]
 
 
-COPIES = 76 + 40 + 94
+COPIES = 242
 ROW_NODES = PIECE * NZ * 2
 COL_NODES = PIECE * NX * NY
 
@@ -576,14 +609,14 @@
     moved = pltpu.make_async_copy(tab_ref, tab_s, tab_sem)
     moved.start()
     moved.wait()
-    product_part(True, ROW_NODES // T, tab_s, masks_ref, xg_ref, rp_ref, pre_ref)
+    form = product_part(True, tab_s, masks_ref, xg_ref, rp_ref, pre_ref)
     plans += dense_part(
-        me, root, rp_ref, weight_ref, bias_ref, cot_ref, hid_ref, gt_ref, gsum_ref,
-        racc_ref, cs_ref, zs_ref, gl_ref, g1_ref, gz_ref, g2_ref,
+        me, root, form, rp_ref, weight_ref, bias_ref, cot_ref, hid_ref, gt_ref, gsum_ref,
+        racc_ref, cs_ref, zs_ref, gl_ref, g1_ref, gz_ref, g2_ref, g3x_ref,
     )
-    product_part(False, COL_NODES // T, tab_s, masks_ref, gt_ref, cp_ref, pre_ref)
+    form = product_part(False, tab_s, masks_ref, gt_ref, cp_ref, pre_ref)
     plans += scatter_part(
-        me, root, cp_ref, gsum_ref, gf_ref, gw_ref, gb_ref, cacc_ref, sum_ref, g3_ref, g3x_ref, g4_ref, yx_ref
+        me, root, form, cp_ref, gsum_ref, gf_ref, gw_ref, gb_ref, cacc_ref, sum_ref, g3_ref, g4_ref, yx_ref
     )
     for plan in plans:
         plan.drain()
@@ -620,9 +653,9 @@
             pltpu.VMEM((16, T), F32),
             pltpu.VMEM((144, T), F32),
             pltpu.VMEM((72, T), F32),
+            pltpu.VMEM((16 * NY, T), F32),
+            pltpu.VMEM((16 * NY, T), F32),
             pltpu.VMEM((16 * NZ, T), F32),
-            pltpu.VMEM((16 * NZ, T), F32),
-            pltpu.VMEM((16 * NY, T), F32),
             pltpu.VMEM((16 * NX, T), F32),
             pltpu.VMEM((T, T), F32),
             pltpu.VMEM((PIECE, T), F32),

time: 104 us -> 99.1 us (0.953)
  Pallas kernels: 99 us -> 94 us
    pallas_call x1, Pallas kernels: 99 us -> 94 us  [local(): pl.pallas_call(body, out_shape=(jax.ShapeDtypeStruct((PIECE, T), BF16), j...]
where the time goes in v4:
time: 99.1 us; the launch traced here: 98.8 us
  Pallas kernels  94 us (95%)
  local copies, waits for them, and re-layouts  3.55 us (4%)
  between operations  1.3 us (1%)
    pallas_call x1, Pallas kernels, local(): pl.pallas_call(body, out_shape=(jax.ShapeDtypeStruct((PIECE, T), BF16), j...  94 us
    unnamed x10, local copies, waits for them, and re-layouts  3.55 us

profile of v4, /device:TPU:1, one launch (start us, length us, event | category | flops | bytes accessed | tf_op | source)
XLA Modules:
  0.0 98.8 jit_solution(14414793743913189957)
XLA Ops:
  1.3 94.0 %layer.1 = (bf16[256,128]{1,0:T(8,128)(2,1)}, bf16[256,128]{1,0:T(8,128)(2,1)}, f32[128,128]{1,0:T(8,128)}, f32[1,128]{1,0:T(1,128)}) custom-call(bf16[256,128]{1,0:T(8,128)(2,1)} %feat_ref.1, s32[2,128]{1,0:T(2,128)} %bitcast.9, bf16[128,128]{1,0:T(8,128)(2,1)} %weight_ref.1, f32[1,128]{1,0:T(1,128)} %bitcast.10, bf16[256,128]{1,0:T(8,128)(2,1)} %cot_ref.1, ...), custom_call_target="tpu_custom_call" | custom-call | tf_op jit(solution)/shard_map/layer/pallas_call | solution.py:628
  95.2 0.0 copy-start.1
  95.3 1.5 %copy.18 = bf16[256,128]{1,0:T(8,128)(2,1)} copy(bf16[256,128]{1,0:T(8,128)(2,1)} %get-tuple-element.16) | data formatting | bytes 131072
  96.8 0.0 copy-done.1
  96.8 0.0 copy-start
  96.8 0.6 copy.19
  97.4 0.2 copy-done
  97.6 0.0 copy-start.2
  97.6 0.6 copy.20
  98.3 0.0 copy-done.2
  98.3 0.5 copy.21
Async XLA Ops:
  95.2 1.5 %copy-start.1 = (bf16[256,128]{1,0:T(8,128)(2,1)S(1)}, bf16[256,128]{1,0:T(8,128)(2,1)}, u32[]{:S(2)}) copy-start(bf16[256,128]{1,0:T(8,128)(2,1)} %get-tuple-element.17) | copy-start | bytes 196612
  96.8 0.9 copy-start
  97.6 0.7 copy-start.2

commit v5 on v4

--- a/solution.py
+++ b/solution.py
@@ -19,7 +19,7 @@
 SLOTS = 128
 PRIME = 4093
 ROUND = 12582912.0
-CUT = 128
+CUT = 96
 
 WIRE = 46e3
 CORE_WIRE = 250e3
@@ -173,11 +173,9 @@
         dst[rows_of(piece, f, n), :] = v.astype(BF16)
 
 
-CHAIN4 = ((0, 1), (1, 1))
 DIRECT4 = ((0, 1), (0, 2))
-CHAIN8 = ((0, 1), (1, 1), (2, 1), (3, 1))
 TWO8 = ((0, 2), (0, 1), (2, 2), (2, 1))
-STEPS = {("A", "x"): DIRECT4, ("A", "y"): TWO8, ("B", "y"): TWO8, ("B", "x"): CHAIN4}
+STEPS = {("A", "x"): DIRECT4, ("A", "y"): TWO8, ("B", "y"): TWO8, ("B", "x"): DIRECT4}
 STEPS_Z = TWO8
 
 
@@ -620,6 +618,11 @@
     )
     for plan in plans:
         plan.drain()
+
+
+def hand_over(*refs):
+    for given, out in zip(refs[:4], refs[4:]):
+        out[...] = given[...]
 
 
 def local(features, degree, weight, bias, cotangent, tile_rows, tile_cols, tile_count, tile_codes):
@@ -677,6 +680,13 @@
         tile_count.reshape(1, 1),
         tile_codes.reshape(SLOTS, 2 * T),
     )
+    hidden, grad_features, grad_weight, grad_bias = pl.pallas_call(
+        hand_over,
+        out_shape=tuple(jax.ShapeDtypeStruct(v.shape, v.dtype) for v in (hidden, grad_features, grad_weight, grad_bias)),
+        in_specs=[vmem] * 4,
+        out_specs=(vmem,) * 4,
+        name="hand_over",
+    )(hidden, grad_features, grad_weight, grad_bias)
     return hidden, grad_features, grad_weight, grad_bias.reshape(T)
 
 

time: 99.1 us -> 96.4 us (0.973)
  local copies, waits for them, and re-layouts: 3.55 us -> 0 us
    unnamed x10 -> x0, local copies, waits for them, and re-layouts: 3.55 us -> none
    pallas_call x0 -> x1, Pallas kernels: none -> 1.59 us  [local(): pl.pallas_call(hand_over, out_shape=tuple((jax.ShapeDtypeStruct(v.shape,...]
where the time goes in v5:
time: 96.4 us; the launch traced here: 96.2 us
  Pallas kernels  94.9 us (98%)
  between operations  1.29 us (1%)
    pallas_call x1, Pallas kernels, local(): pl.pallas_call(body, out_shape=(jax.ShapeDtypeStruct((PIECE, T), BF16), j...  93.3 us

profile of v5, /device:TPU:1, one launch (start us, length us, event | category | flops | bytes accessed | tf_op | source)
XLA Modules:
  0.0 96.2 jit_solution(16470301149658470935)
XLA Ops:
  1.3 93.3 %layer.1 = (bf16[256,128]{1,0:T(8,128)(2,1)}, bf16[256,128]{1,0:T(8,128)(2,1)}, f32[128,128]{1,0:T(8,128)}, f32[1,128]{1,0:T(1,128)}) custom-call(bf16[256,128]{1,0:T(8,128)(2,1)} %feat_ref.1, s32[2,128]{1,0:T(2,128)} %bitcast.9, bf16[128,128]{1,0:T(8,128)(2,1)} %weight_ref.1, f32[1,128]{1,0:T(1,128)} %bitcast.10, bf16[256,128]{1,0:T(8,128)(2,1)} %cot_ref.1, ...), custom_call_target="tpu_custom_call" | custom-call | tf_op jit(solution)/shard_map/layer/pallas_call | solution.py:631
  94.6 1.6 %hand_over.1 = (bf16[256,128]{1,0:T(8,128)(2,1)}, bf16[256,128]{1,0:T(8,128)(2,1)}, f32[128,128]{1,0:T(8,128)}, f32[1,128]{1,0:T(1,128)}) custom-call(bf16[256,128]{1,0:T(8,128)(2,1)} %get-tuple-element.12.refs_0_, bf16[256,128]{1,0:T(8,128)(2,1)} %get-tuple-element.13.refs_1_, f32[128,128]{1,0:T(8,128)} %get-tuple-element.14.refs_2_, ...), custom_call_target="tpu_custom_call" | custom-call | tf_op jit(solution)/shard_map/hand_over/pallas_call | solution.py:683
